TPU v7x, 32 devices: a whole 2x2x4 slice. The times are simulated.
32 devices in a mesh: groups: 2 (over y), head: 4 (over z), state: 4 (over x, core).
Axes of the slice: x: 2, y: 2, z: 4, core: 2. Of those that a mesh axis runs over, the one named last changes fastest.
Arguments:
- tokens: bfloat16 [32, 2048], P(('groups', 'head'), 'state'), parts along dimension 0, may hold values from -20 to 20
- mixer_norm: float32 [2048], P('state'), may hold values from 0.1 to 1.9
- input_proj: bfloat16 [2, 2048, 8192], P(None, 'state', 'head'), may hold values from -0.125 to 0.125
- conv_weight: float32 [4, 8192], P(None, 'head'), may hold values from -3 to 3
- conv_bias: float32 [8192], P('head'), may hold values from -3 to 3
- conv_state: float32 [3, 32, 8192], P(None, 'groups', 'head'), parts along dimension 1, may hold values from -6 to 6
- state_proj: bfloat16 [8192, 288], P('head'), may hold values from -0.125 to 0.125
- step_gain: float32 [256], replicated, may hold values from 0.1 to 1.9
- step_proj: bfloat16 [256, 8192], P(None, 'head'), may hold values from -0.375 to 0.375
- step_bias: float32 [8192], P('head'), may hold values from -6 to -1
- decay_log: float32 [16, 8192], P('state', 'head'), may hold values from 0 to 2.77
- skip_gain: float32 [8192], P('head'), may hold values from 0.5 to 1.5
- ssm_state: float32 [16, 32, 8192], P('state', 'groups', 'head'), parts along dimension 1, may hold values from -6 to 6
- output_proj: bfloat16 [8192, 2048], P('head', 'state'), may hold values from -0.0625 to 0.0625
- moe_norm: float32 [2048], replicated, may hold values from 0.1 to 1.9
- router_weight: float32 [2048, 8], replicated, may hold values from -0.125 to 0.125
- expert_ids: int32 [32, 2], P(('groups', 'head')), parts along dimension 0, may hold values from 0 to 7, as said below
- slot_ids: int32 [32, 2], P(('groups', 'head')), parts along dimension 0, may hold values from 0 to 3, as said below
- gate_proj: bfloat16 [8, 2048, 7168], P('head', None, 'state'), may hold values from -0.125 to 0.125
- up_proj: bfloat16 [8, 2048, 7168], P('head', None, 'state'), may hold values from -0.125 to 0.125
- down_proj: bfloat16 [8, 7168, 2048], P('head', 'state'), may hold values from -0.0625 to 0.0625
Outputs:
- layer_out: bfloat16 [32, 2048], P(('groups', 'head'), 'state'), parts along dimension 0
- new_conv: float32 [3, 32, 8192], P(None, 'groups', 'head'), parts along dimension 1
- new_state: float32 [16, 32, 8192], P('state', 'groups', 'head'), parts along dimension 1
- expert_load: float32 [16], P('groups'), parts along dimension 0
- aux_loss: float32 [2], P('groups'), parts along dimension 0
There are 2 independent parts, one for each index of `groups`. A program takes and returns all parts, laid end to end along the dimension named above; an argument that names none is the same for every part. Nothing has to cross between parts.
Inputs may be any that keep to these rules, and one draw needn't show every extreme that they name: `expert_ids`: each row names 2 different experts. One expert, the same on every device, is named by every row. `slot_ids`: among the choices of one aligned block of 4 rows that name one expert, the slot positions are distinct and run from 0 to their count less one.
All inputs are finite; a program needn't handle non-finite values.
Results may differ from a plain program's by a relative error of at most 0.007.
Values may be sent and summed in bfloat16 or wider, within the bound.
No kernel may reach another device: no remote copies, remote signals or barrier semaphores. Data moves between devices by JAX's collectives and lax.ppermute only.
A program may use at most 128 MiB of HBM per device.

v0:
```python
import jax
import jax.numpy as jnp
from jax import lax
from jax.sharding import PartitionSpec as P

D = 2048
D_STATE = 16
DT_RANK = 256
EXPERTS = 8
TOPK = 2
CAP = 2


NORM_EPS = 1e-05
STEP_EPS = 1e-06


def expert_ffn(received, gate_proj, up_proj, down_proj):
    gate_val = jnp.einsum("nlcd,ldf->nlcf", received, gate_proj, preferred_element_type=jnp.float32)
    up_val = jnp.einsum("nlcd,ldf->nlcf", received, up_proj, preferred_element_type=jnp.float32)
    hidden = (jax.nn.silu(gate_val) * up_val).astype(jnp.bfloat16)
    return jnp.einsum("nlcf,lfd->nlcd", hidden, down_proj, preferred_element_type=jnp.float32)


def per_device(
    tokens,
    mixer_norm,
    input_proj,
    conv_weight,
    conv_bias,
    conv_state,
    state_proj,
    step_gain,
    step_proj,
    step_bias,
    decay_log,
    skip_gain,
    ssm_state,
    output_proj,
    moe_norm,
    router_weight,
    expert_ids,
    slot_ids,
    gate_proj,
    up_proj,
    down_proj,
):
    head_count = lax.axis_size("head")
    state_index = lax.axis_index("state")
    own_rows = tokens.shape[0]
    tok_f32 = tokens.astype(jnp.float32)
    first_sq = lax.psum(jnp.sum(tok_f32 * tok_f32, axis=1), "state")
    inv_first = lax.rsqrt(first_sq / D + NORM_EPS)[:, None]
    normed = (tok_f32 * inv_first * mixer_norm).astype(jnp.bfloat16)
    branch_part = jnp.einsum(
        "td,kdc->ktc",
        lax.all_gather(normed, "head", axis=0, tiled=True),
        input_proj,
        preferred_element_type=jnp.float32,
    )
    branch_full = lax.psum(branch_part, "state")
    conv_input = branch_full[0]
    gate_branch = branch_full[1]
    window = jnp.concatenate([conv_state, conv_input[None]], axis=0)
    conv_out = jax.nn.silu(jnp.sum(conv_weight[:, None, :] * window, axis=0) + conv_bias)
    new_conv = window[1:]
    proj_part = jnp.dot(
        conv_out.astype(jnp.bfloat16), state_proj, preferred_element_type=jnp.float32
    )
    projected = lax.psum(proj_part, "head")
    step_low = projected[:, :DT_RANK]
    state_slab = decay_log.shape[0]
    b_input = lax.dynamic_slice_in_dim(projected, DT_RANK + state_index * state_slab, state_slab, 1)
    c_output = lax.dynamic_slice_in_dim(
        projected, DT_RANK + D_STATE + state_index * state_slab, state_slab, 1
    )
    step_inv = lax.rsqrt(jnp.mean(step_low * step_low, axis=1, keepdims=True) + STEP_EPS)
    step_normed = (step_low * step_inv * step_gain).astype(jnp.bfloat16)
    step_size = jax.nn.softplus(
        jnp.dot(step_normed, step_proj, preferred_element_type=jnp.float32) + step_bias
    )
    decay_rate = jnp.exp(-step_size[None] * jnp.exp(decay_log)[:, None, :])
    new_state = decay_rate * ssm_state + step_size[None] * b_input.T[:, :, None] * conv_out[None]
    read_part = jnp.sum(c_output.T[:, :, None] * new_state, axis=0)
    readout = lax.psum(read_part, "state")
    mixer_act = ((readout + skip_gain * conv_out) * jax.nn.silu(gate_branch)).astype(jnp.bfloat16)
    mixer_sum = lax.psum_scatter(
        jnp.dot(mixer_act, output_proj, preferred_element_type=jnp.float32),
        "head",
        scatter_dimension=0,
        tiled=True,
    )
    residual = (tok_f32 + mixer_sum).astype(jnp.bfloat16)
    full_rows = lax.all_gather(residual, "state", axis=1, tiled=True).astype(jnp.float32)
    inv_second = lax.rsqrt(jnp.mean(full_rows * full_rows, axis=1, keepdims=True) + NORM_EPS)
    scaled = full_rows * moe_norm
    logits = inv_second * jnp.dot(scaled, router_weight, precision=lax.Precision.HIGHEST)
    row_normed = (scaled * inv_second).astype(jnp.bfloat16)
    expert_hit = expert_ids[:, :, None] == jnp.arange(EXPERTS, dtype=jnp.int32)[None, None, :]
    chosen = jnp.sum(jnp.where(expert_hit, logits[:, None, :], 0.0), axis=2)
    gate_probs = jax.nn.sigmoid(chosen - chosen[:, ::-1])
    kept_mask = slot_ids < CAP
    mix_weight = jnp.where(kept_mask, gate_probs, 0.0)
    slot_hit = slot_ids[:, :, None] == jnp.arange(CAP, dtype=jnp.int32)[None, None, :]
    slot_place = expert_hit[:, :, :, None] & slot_hit[:, :, None, :]
    dispatch = jnp.sum(slot_place.astype(jnp.int32), axis=1).astype(jnp.bfloat16)
    combine_weight = jnp.sum(jnp.where(slot_place, mix_weight[:, :, None, None], 0.0), axis=1)
    outgoing = jnp.einsum(
        "tec,td->ecd", dispatch, row_normed, preferred_element_type=jnp.float32
    ).astype(jnp.bfloat16)
    row_width = outgoing.shape[2]
    local_experts = gate_proj.shape[0]
    expert_groups = EXPERTS // local_experts
    copies = head_count * local_experts // EXPERTS
    outgoing = jnp.broadcast_to(
        outgoing.reshape(expert_groups, 1, local_experts, CAP, row_width),
        (expert_groups, copies, local_experts, CAP, row_width),
    )
    outgoing = outgoing.reshape(head_count, local_experts, CAP, row_width)
    partial_out = expert_ffn(
        lax.all_to_all(outgoing, "head", split_axis=0, concat_axis=0, tiled=True),
        gate_proj,
        up_proj,
        down_proj,
    )
    returned = lax.all_to_all(
        partial_out.astype(jnp.bfloat16), "head", split_axis=0, concat_axis=0, tiled=True
    ).astype(partial_out.dtype)
    per_expert = returned.reshape(expert_groups, copies, local_experts, CAP, row_width).sum(axis=1)
    per_expert = per_expert.reshape(EXPERTS, CAP, row_width)
    expert_mix = jnp.einsum(
        "tec,ecd->td", combine_weight, per_expert, precision=lax.Precision.HIGHEST
    )
    expert_mix = lax.psum_scatter(
        expert_mix.astype(jnp.bfloat16), "state", scatter_dimension=1, tiled=True
    ).astype(jnp.float32)
    layer_out = (residual.astype(jnp.float32) + expert_mix).astype(jnp.bfloat16)
    load_own = jnp.sum(jnp.where(expert_hit & kept_mask[:, :, None], 1.0, 0.0), axis=(0, 1)).astype(
        jnp.float32
    )
    prob_own = jnp.sum(jax.nn.sigmoid(logits), axis=0)
    load_sum, prob_sum = lax.psum((load_own, prob_own), "head")
    total_rows = head_count * own_rows
    aux_value = EXPERTS * jnp.sum(load_sum / (total_rows * TOPK) * (prob_sum / total_rows))
    return (layer_out, new_conv, new_state, load_sum, aux_value.reshape(1))


def solution(mesh):
    return jax.shard_map(
        per_device,
        mesh=mesh,
        in_specs=(
            P(("groups", "head"), "state"),
            P("state"),
            P(None, "state", "head"),
            P(None, "head"),
            P("head"),
            P(None, "groups", "head"),
            P("head", None),
            P(),
            P(None, "head"),
            P("head"),
            P("state", "head"),
            P("head"),
            P("state", "groups", "head"),
            P("head", "state"),
            P(),
            P(),
            P(("groups", "head"), None),
            P(("groups", "head"), None),
            P("head", None, "state"),
            P("head", None, "state"),
            P("head", "state", None),
        ),
        out_specs=(
            P(("groups", "head"), "state"),
            P(None, "groups", "head"),
            P("state", "groups", "head"),
            P("groups"),
            P("groups"),
        ),
        check_vma=False,
    )
```

profile of v0, /device:TPU:0, one launch (start us, length us, event | category | flops | bytes accessed | tf_op | source)
XLA Modules:
  0.0 225.7 jit_solution(13633011839943154887)
XLA Ops:
  8.2 8.4 %psum.42 = f32[4]{0:T(128)S(1)} all-reduce(f32[4]{0:T(128)S(1)} %fusion.46), channel_id=1, replica_groups=mesh['groups'=2,'head'=4,'state'=4] {'state'}, use_global_device_ids=true, to_apply=%region_1.0 | all-reduce | flops 4 | bytes 32 | tf_op jit(solution)/shard_map/psum | solution.py:52
  17.4 13.4 %all-gather = bf16[4,4,512]{2,1,0:T(4,128)(2,1)S(1)} all-gather(bf16[1,4,512]{2,1,0:T(4,128)(2,1)S(1)} %fusion.52), channel_id=1, replica_groups=mesh['groups'=2,'head'=4,'state'=4] {'head'}, dimensions={0}, use_global_device_ids=true | all-gather | bytes 20480 | tf_op jit(solution)/shard_map/all_gather | solution.py:57
  30.8 3.6 %convolution_bitcast_fusion = f32[2,16,2048]{2,1,0:T(8,128)} fusion(bf16[16,512,1]{1,0,2:T(8,128)(2,1)S(1)} %reshape.86, bf16[2,512,2048]{2,1,0:T(8,128)(2,1)} %param.23), kind=kOutput, calls=%fused_computation.6 | convolution fusion | flops 67108864 | bytes 4472832 | tf_op jit(solution)/shard_map/td,kdc->ktc/dot_general | solution.py:55
  37.3 1.2 dynamic-slice
  39.3 27.6 %all-reduce.5.cloned.1.call-done = f32[2,16,2048]{2,1,0:T(8,128)} async-done(((f32[2,16,2048]{2,1,0:T(8,128)}), f32[2,16,2048]{2,1,0:T(8,128)}) %all-reduce.5.cloned.1.call-update) | async-done | bytes 262160 | tf_op jit(solution)/shard_map/psum | solution.py:61
  67.8 1.1 fusion.26
  69.6 1.7 fusion.31
  71.3 19.0 %psum.44 = f32[16,288]{1,0:T(8,128)S(1)} all-reduce(f32[16,288]{1,0:T(8,128)S(1)} %fusion.31), channel_id=1, replica_groups=mesh['groups'=2,'head'=4,'state'=4] {'head'}, use_global_device_ids=true, to_apply=%region_4.5 | all-reduce | flops 4608 | bytes 36864 | tf_op jit(solution)/shard_map/psum | solution.py:70
  90.7 1.5 fusion.56
  92.2 2.7 %multiply_reduce_fusion = (f32[16,2048]{1,0:T(8,128)}, f32[4,16,2048]{2,1,0:T(8,128)}) fusion(f32[4,16]{1,0:T(4,128)S(1)} %copy.53, f32[16,2048]{1,0:T(8,128)S(1)} %divide_multiply_fusion, f32[4,16]{1,0:T(4,128)S(1)} %copy.54, f32[16,2048]{1,0:T(8,128)S(1)} %get-tuple-element.14, f32[4,16,2048]{2,1,0:T(8,128)} %param.33, f32[4,2048]{1,0:T(4,128)S(1)} %exp.33, ...), kind=kLoop, calls=%fused_computation.23 | loop fusion | flops 884736 | bytes 1606144 | tf_op jit(solution)/shard_map/reduce_sum | solution.py:84
  94.9 1.7 fusion.27
  96.6 27.5 %all-reduce.7.cloned.1.call-done = f32[16,2048]{1,0:T(8,128)} async-done(((f32[16,2048]{1,0:T(8,128)}), f32[16,2048]{1,0:T(8,128)}) %all-reduce.7.cloned.1.call-update) | async-done | bytes 131088 | tf_op jit(solution)/shard_map/psum | solution.py:85
  124.1 1.3 fusion.28
  125.5 19.0 %all-reduce = f32[16,512]{1,0:T(8,128)S(1)} all-reduce(f32[16,512]{1,0:T(8,128)S(1)} %fusion.28), channel_id=2, replica_groups=mesh['groups'=2,'head'=4,'state'=4] {'head'}, use_global_device_ids=true, to_apply=%region_8.9.clone | all-reduce | flops 8192 | bytes 65536
  145.2 5.2 %all_gather.7 = bf16[4,2048]{1,0:T(4,128)(2,1)S(1)} all-gather(bf16[4,512]{1,0:T(4,128)(2,1)S(1)} %fusion.49), channel_id=1, replica_groups=mesh['groups'=2,'head'=4,'state'=4] {'state'}, dimensions={1}, use_global_device_ids=true | all-gather | bytes 20480 | tf_op jit(solution)/shard_map/all_gather | solution.py:94
  150.5 1.1 fusion.54
  153.2 3.3 %all-to-all-start = ((bf16[4,2,2,2048]{3,2,1,0:T(2,128)(2,1)}), bf16[4,2,2,2048]{3,2,1,0:T(2,128)(2,1)S(1)}, u32[]{:S(2)}, u32[]{:S(2)}) async-start(bf16[4,2,2,2048]{3,2,1,0:T(2,128)(2,1)} %bitcast.6), calls=%async_computation | async-start | bytes 131072 | tf_op jit(solution)/shard_map/all_to_all | solution.py:121
  156.7 12.1 %all-reduce.1 = (f32[8]{0:T(128)S(1)}, f32[8]{0:T(128)S(1)}) all-reduce(f32[8]{0:T(128)S(1)} %get-tuple-element.5, f32[8]{0:T(128)S(1)} %get-tuple-element.15), channel_id=1, replica_groups=mesh['groups'=2,'head'=4,'state'=4] {'head'}, use_global_device_ids=true, to_apply=%region_15.16 | all-reduce | flops 16 | bytes 128 | tf_op jit(solution)/shard_map/psum | solution.py:142
  168.9 7.5 %fusion.6 = f32[4,2,2,1792]{3,0,2,1:T(4,128)S(1)} fusion(bf16[2,2048,1792]{2,1,0:T(8,128)(2,1)} %param.39, bf16[4,2,2,2048]{3,2,1,0:T(2,128)(2,1)S(1)} %all-to-all-done), kind=kOutput, calls=%fused_computation.7 | convolution fusion | flops 117440512 | bytes 14860288 | tf_op jit(solution)/shard_map/nlcd,ldf->nlcf/dot_general | solution.py:19
  176.4 7.5 %fusion.15 = bf16[4,2,2,1792]{3,0,2,1:T(4,128)(2,1)S(1)} fusion(bf16[2,2048,1792]{2,1,0:T(8,128)(2,1)} %param.40, f32[4,2,2,1792]{3,0,2,1:T(4,128)S(1)} %fusion.6, bf16[4,2,2,2048]{3,2,1,0:T(2,128)(2,1)S(1)} %all-to-all-done), kind=kOutput, calls=%fused_computation.11 | convolution fusion | flops 117612544 | bytes 14917632 | tf_op jit(solution)/shard_map/nlcd,ldf->nlcf/dot_general | solution.py:20
  183.9 2.1 fusion.21
  186.7 3.3 %all-to-all-start.1 = ((bf16[4,2,2,2048]{3,2,1,0:T(2,128)(2,1)}), bf16[4,2,2,2048]{3,2,1,0:T(2,128)(2,1)S(1)}, u32[]{:S(2)}, u32[]{:S(2)}) async-start(bf16[4,2,2,2048]{3,2,1,0:T(2,128)(2,1)} %copy.58), calls=%async_computation.1 | async-start | bytes 131072 | tf_op jit(solution)/shard_map/all_to_all | solution.py:126
  190.1 5.6 %all-to-all-done.1 = bf16[4,2,2,2048]{3,2,1,0:T(2,128)(2,1)S(1)} async-done(((bf16[4,2,2,2048]{3,2,1,0:T(2,128)(2,1)}), bf16[4,2,2,2048]{3,2,1,0:T(2,128)(2,1)S(1)}, u32[]{:S(2)}, u32[]{:S(2)}) %all-to-all-start.1) | async-done | bytes 65568 | tf_op jit(solution)/shard_map/all_to_all | solution.py:126
  198.3 18.1 %reduce-scatter.4.cloned.1.call-done = bf16[512,4]{1,0:T(8,128)(2,1)} async-done(((bf16[2048,4]{1,0:T(8,128)(2,1)}), bf16[512,4]{1,0:T(8,128)(2,1)}) %reduce-scatter.4.cloned.1.call-update) | async-done | bytes 4112
  (55 shorter events, 13.9 us)
Async XLA Ops:
  7.2 117.0 %copy-start = (bf16[2048,512]{1,0:T(8,128)(2,1)S(1)}, bf16[2048,512]{1,0:T(8,128)(2,1)}, u32[]{:S(2)}) copy-start(bf16[2048,512]{1,0:T(8,128)(2,1)} %param.34) | copy-start | bytes 6291460
  7.2 149.4 %copy-start.1 = (s32[4,2]{0,1:T(2,128)S(1)}, s32[4,2]{0,1:T(2,128)}, u32[]{:S(2)}) copy-start(s32[4,2]{0,1:T(2,128)} %param.37) | copy-start | bytes 100
  7.2 149.5 %copy-start.2 = (s32[4,2]{0,1:T(2,128)S(1)}, s32[4,2]{0,1:T(2,128)}, u32[]{:S(2)}) copy-start(s32[4,2]{0,1:T(2,128)} %param.38) | copy-start | bytes 100
  7.2 59.7 %all-reduce.5.cloned.1.call-start = ((), (), s32[]{:S(2)}) async-start(), calls=%async_computation.3 | async-start | bytes 524288 | tf_op jit(solution)/shard_map/psum | solution.py:61
  34.4 89.8 %all-reduce.7.cloned.1.call-start = ((), (), s32[]{:S(2)}) async-start(), calls=%async_computation.4 | async-start | bytes 262144 | tf_op jit(solution)/shard_map/psum | solution.py:85
  153.2 15.7 %all-to-all-start = ((bf16[4,2,2,2048]{3,2,1,0:T(2,128)(2,1)}), bf16[4,2,2,2048]{3,2,1,0:T(2,128)(2,1)S(1)}, u32[]{:S(2)}, u32[]{:S(2)}) async-start(bf16[4,2,2,2048]{3,2,1,0:T(2,128)(2,1)} %bitcast.6), calls=%async_computation | async-start | bytes 131072 | tf_op jit(solution)/shard_map/all_to_all | solution.py:121
  168.9 28.1 %copy-start.3 = (f32[8]{0:T(128)}, f32[8]{0:T(128)S(1)}, u32[]{:S(2)}) copy-start(f32[8]{0:T(128)S(1)} %get-tuple-element.7) | copy-start | bytes 100
  168.9 15.0 %slice-start = ((s8[14680064]{0:T(1024)(128)(4,1)}), s8[4194304]{0:T(1024)(128)(4,1)S(1)}, s32[]{:S(2)}) async-start(s8[14680064]{0:T(1024)(128)(4,1)} %bitcast.71), calls=%async_computation.6 | async-start | bytes 8388608
  168.9 15.0 %slice-start.1 = ((s8[14680064]{0:T(1024)(128)(4,1)}), s8[4194304]{0:T(1024)(128)(4,1)S(1)}, s32[]{:S(2)}) async-start(s8[14680064]{0:T(1024)(128)(4,1)} %bitcast.71), calls=%async_computation.7 | async-start | bytes 8388608
  176.4 7.5 %slice-start.2 = ((s8[14680064]{0:T(1024)(128)(4,1)}), s8[4194304]{0:T(1024)(128)(4,1)S(1)}, s32[]{:S(2)}) async-start(s8[14680064]{0:T(1024)(128)(4,1)} %bitcast.71), calls=%async_computation.8 | async-start | bytes 8388608
  176.4 7.5 %slice-start.3 = ((s8[14680064]{0:T(1024)(128)(4,1)}), s8[2097152]{0:T(1024)(128)(4,1)S(1)}, s32[]{:S(2)}) async-start(s8[14680064]{0:T(1024)(128)(4,1)} %bitcast.71), calls=%async_computation.9 | async-start | bytes 4194304
  186.7 9.0 %all-to-all-start.1 = ((bf16[4,2,2,2048]{3,2,1,0:T(2,128)(2,1)}), bf16[4,2,2,2048]{3,2,1,0:T(2,128)(2,1)S(1)}, u32[]{:S(2)}, u32[]{:S(2)}) async-start(bf16[4,2,2,2048]{3,2,1,0:T(2,128)(2,1)} %copy.58), calls=%async_computation.1 | async-start | bytes 131072 | tf_op jit(solution)/shard_map/all_to_all | solution.py:126
  190.0 26.4 %reduce-scatter.4.cloned.1.call-start = ((), (), s32[]{:S(2)}) async-start(), calls=%async_computation.5 | async-start | bytes 655360
Sparse Core Ops, SparseCore 0:
  34.5 32.3 all-reduce.4
  95.0 29.0 all-reduce.6
  197.2 19.2 reduce-scatter.3
where the time goes:
time: 227 us; the launch traced here: 226 us
  waiting for transfers between devices  78.8 us (35%)
  blocking collectives  77.1 us (34%)
  matrix products  27.5 us (12%)
  between operations  16.4 us (7%)
  other arithmetic  12.6 us (6%)
  local copies, waits for them, and re-layouts  6.69 us (3%)
  starting transfers between devices  6.69 us (3%)
    psum x1, waiting for transfers between devices, per_device(): branch_full = lax.psum(branch_part, 'state')  27.6 us
    psum x1, waiting for transfers between devices, per_device(): readout = lax.psum(read_part, 'state')  27.5 us
    unnamed x1, blocking collectives  19 us
    psum x1, blocking collectives, per_device(): projected = lax.psum(proj_part, 'head')  19 us
    unnamed x4, waiting for transfers between devices  18.2 us
    all_gather x1, blocking collectives, per_device(): lax.all_gather(normed, 'head', axis=0, tiled=True)  13.4 us
    psum x1, blocking collectives, per_device(): load_sum, prob_sum = lax.psum((load_own, prob_own), 'head')  12.1 us
    psum x1, blocking collectives, per_device(): first_sq = lax.psum(jnp.sum(tok_f32 * tok_f32, axis=1), 'state')  8.36 us
  transfers between devices with their start and end apart: 5, of which 4 were waited for; matrix products, arithmetic and copies ran while one was open for 3% of the time, Pallas kernels for 0%

commit v1 on v0

v1 whole, which is shorter than its diff:
```python
import jax
import jax.numpy as jnp
from jax import lax
from jax.sharding import PartitionSpec as P

TOPK = 2
CAP = 2

NORM_EPS = 1e-05
STEP_EPS = 1e-06
LANES = 128
BF16 = jnp.bfloat16
F32 = jnp.float32


def gather_rows(block, axis):
    count = lax.axis_size(axis)
    if count > 8:
        return lax.all_gather(block, axis, axis=0, tiled=True)
    spread = jnp.broadcast_to(block[None], (count, *block.shape))
    spread = lax.all_to_all(spread, axis, split_axis=0, concat_axis=0, tiled=True)
    return spread.reshape(count * block.shape[0], *block.shape[1:])


def exchange_sum(part, axis, dtype):
    count = lax.axis_size(axis)
    if count != 4:
        return lax.psum(part, axis)
    sent = part.astype(dtype)
    others = [
        lax.ppermute(sent, axis, [(i, i ^ k) for i in range(count)]).astype(F32)
        for k in range(1, count)
    ]
    return (sent.astype(F32) + others[0]) + (others[1] + others[2])


def per_device(
    tokens,
    mixer_norm,
    input_proj,
    conv_weight,
    conv_bias,
    conv_state,
    state_proj,
    step_gain,
    step_proj,
    step_bias,
    decay_log,
    skip_gain,
    ssm_state,
    output_proj,
    moe_norm,
    router_weight,
    expert_ids,
    slot_ids,
    gate_proj,
    up_proj,
    down_proj,
):
    head_count = lax.axis_size("head")
    state_count = lax.axis_size("state")
    head_index = lax.axis_index("head")
    state_index = lax.axis_index("state")
    own_rows, own_cols = tokens.shape
    model_width = moe_norm.shape[0]
    experts = router_weight.shape[1]
    dt_rank = step_gain.shape[0]
    state_slab = decay_log.shape[0]
    d_state = state_slab * state_count
    channels = conv_bias.shape[0]

    routing = jnp.concatenate([expert_ids, jnp.minimum(slot_ids, CAP)], axis=1).astype(BF16)
    routing = jnp.pad(routing, ((0, 0), (0, LANES - 2 * TOPK)))
    packed = gather_rows(jnp.concatenate([tokens, routing], axis=1), "head")
    tok_all = packed[:, :own_cols]
    rows = tok_all.shape[0]
    expert_all = packed[:, own_cols : own_cols + TOPK].astype(jnp.int32)
    kept_all = packed[:, own_cols + TOPK : own_cols + 2 * TOPK].astype(F32) < CAP

    tok_f32 = tok_all.astype(F32)
    sq_part = jnp.sum(tok_f32 * tok_f32, axis=1, keepdims=True)
    sq_high = sq_part.astype(BF16)
    sq_low = (sq_part - sq_high.astype(F32)).astype(BF16)
    tok_gained = (tok_f32 * mixer_norm).astype(BF16)
    branch_part = jnp.einsum("td,kdc->ktc", tok_gained, input_proj, preferred_element_type=F32)
    extra = jnp.pad(jnp.concatenate([sq_high, sq_low], axis=1), ((0, 0), (0, LANES - 2)))
    extra = jnp.broadcast_to(extra[None], (2, rows, LANES))
    branch_sent = jnp.concatenate([branch_part.astype(BF16), extra], axis=2)
    branch_all = lax.all_gather(branch_sent, "state").astype(F32)
    branch_full = jnp.sum(branch_all, axis=0)
    first_sq = branch_full[0, :, channels : channels + 1] + branch_full[0, :, channels + 1 : channels + 2]
    inv_first = lax.rsqrt(first_sq / model_width + NORM_EPS)
    conv_input = branch_full[0, :, :channels] * inv_first
    gate_branch = branch_full[1, :, :channels] * inv_first
    window = jnp.concatenate([conv_state, conv_input[None]], axis=0)
    conv_out = jax.nn.silu(jnp.sum(conv_weight[:, None, :] * window, axis=0) + conv_bias)
    new_conv = window[1:]

    proj_part = jnp.dot(conv_out.astype(BF16), state_proj, preferred_element_type=F32)
    projected = exchange_sum(proj_part, "head", F32)
    step_low = projected[:, :dt_rank]
    b_input = lax.dynamic_slice_in_dim(projected, dt_rank + state_index * state_slab, state_slab, 1)
    c_output = lax.dynamic_slice_in_dim(
        projected, dt_rank + d_state + state_index * state_slab, state_slab, 1
    )
    step_inv = lax.rsqrt(jnp.mean(step_low * step_low, axis=1, keepdims=True) + STEP_EPS)
    step_normed = (step_low * step_inv * step_gain).astype(BF16)
    step_size = jax.nn.softplus(
        jnp.dot(step_normed, step_proj, preferred_element_type=F32) + step_bias
    )
    decay_rate = jnp.exp(-step_size[None] * jnp.exp(decay_log)[:, None, :])
    new_state = decay_rate * ssm_state + step_size[None] * b_input.T[:, :, None] * conv_out[None]
    read_part = jnp.sum(c_output.T[:, :, None] * new_state, axis=0)
    readout = jnp.sum(lax.all_gather(read_part.astype(BF16), "state").astype(F32), axis=0)
    mixer_act = ((readout + skip_gain * conv_out) * jax.nn.silu(gate_branch)).astype(BF16)

    mixer_sum = exchange_sum(
        jnp.dot(mixer_act, output_proj, preferred_element_type=F32), "head", BF16
    )
    resid_cols = (tok_f32 + mixer_sum).astype(BF16)
    resid_all = lax.all_gather(resid_cols, "state", axis=1, tiled=True).astype(F32)
    inv_second = lax.rsqrt(jnp.mean(resid_all * resid_all, axis=1, keepdims=True) + NORM_EPS)
    scaled = resid_all * moe_norm
    row_normed = (scaled * inv_second).astype(BF16)

    gate_val = jnp.einsum("td,ldf->ltf", row_normed, gate_proj, preferred_element_type=F32)
    up_val = jnp.einsum("td,ldf->ltf", row_normed, up_proj, preferred_element_type=F32)
    hidden = (jax.nn.silu(gate_val) * up_val).astype(BF16)
    value = jnp.einsum("ltf,lfd->ltd", hidden, down_proj, preferred_element_type=F32)

    logits = inv_second * jnp.dot(scaled, router_weight, precision=lax.Precision.HIGHEST)
    expert_hit = expert_all[:, :, None] == jnp.arange(experts, dtype=jnp.int32)[None, None, :]
    chosen = jnp.sum(jnp.where(expert_hit, logits[:, None, :], 0.0), axis=2)
    gate_probs = jax.nn.sigmoid(chosen - chosen[:, ::-1])
    mix_weight = jnp.where(kept_all, gate_probs, 0.0)
    local_experts = gate_proj.shape[0]
    split = head_count * local_experts // experts
    own_experts = (head_index * local_experts + jnp.arange(local_experts, dtype=jnp.int32)) // split
    own_hit = expert_all[None, :, :] == own_experts[:, None, None]
    own_weight = jnp.sum(jnp.where(own_hit, mix_weight[None], 0.0), axis=2)
    mix_part = jnp.sum(own_weight[:, :, None] * value, axis=0).astype(BF16)

    outgoing = mix_part.reshape(head_count, own_rows, state_count, own_cols)
    outgoing = outgoing.transpose(0, 2, 1, 3).reshape(head_count * state_count, own_rows, own_cols)
    returned = lax.all_to_all(
        outgoing, ("head", "state"), split_axis=0, concat_axis=0, tiled=True
    )
    expert_mix = jnp.sum(returned.astype(F32), axis=0)
    resid_own = lax.dynamic_slice_in_dim(resid_cols, head_index * own_rows, own_rows, 0)
    layer_out = (resid_own.astype(F32) + expert_mix).astype(BF16)

    load_sum = jnp.sum(jnp.where(expert_hit & kept_all[:, :, None], 1.0, 0.0), axis=(0, 1)).astype(
        F32
    )
    prob_sum = jnp.sum(jax.nn.sigmoid(logits), axis=0)
    aux_value = experts * jnp.sum(load_sum / (rows * TOPK) * (prob_sum / rows))
    return (layer_out, new_conv, new_state, load_sum, aux_value.reshape(1))


def solution(mesh):
    return jax.shard_map(
        per_device,
        mesh=mesh,
        in_specs=(
            P(("groups", "head"), "state"),
            P("state"),
            P(None, "state", "head"),
            P(None, "head"),
            P("head"),
            P(None, "groups", "head"),
            P("head", None),
            P(),
            P(None, "head"),
            P("head"),
            P("state", "head"),
            P("head"),
            P("state", "groups", "head"),
            P("head", "state"),
            P(),
            P(),
            P(("groups", "head"), None),
            P(("groups", "head"), None),
            P("head", None, "state"),
            P("head", None, "state"),
            P("head", "state", None),
        ),
        out_specs=(
            P(("groups", "head"), "state"),
            P(None, "groups", "head"),
            P("state", "groups", "head"),
            P("groups"),
            P("groups"),
        ),
        check_vma=False,
    )
```

time: 227 us -> 98.7 us (0.43)
  waiting for transfers between devices: 78.8 us -> 12.6 us
  blocking collectives: 77.1 us -> 18.4 us
  between operations: 16.4 us -> 2.71 us
  starting transfers between devices: 6.69 us -> 18.6 us
  local copies, waits for them, and re-layouts: 6.69 us -> 10.3 us
  matrix products: 27.5 us -> 24.8 us
    psum x2 -> x0, waiting for transfers between devices: 55.1 us -> none  [the longest x1 27.6 us: per_device(): branch_full = lax.psum(branch_part, 'state')]
    psum x3 -> x0, blocking collectives: 39.5 us -> none  [the longest x1 19 us: per_device(): projected = lax.psum(proj_part, 'head')]
    unnamed x1 -> x0, blocking collectives: 19 us -> none
    unnamed x4 -> x0, waiting for transfers between devices: 18.2 us -> none
    ppermute x0 -> x6, starting transfers between devices: none -> 8.78 us  [exchange_sum(): lax.ppermute(sent, axis, [(i, i ^ k) for i in range(count)]).astype(F32)]
    ppermute x0 -> x6, waiting for transfers between devices: none -> 4.12 us  [exchange_sum(): lax.ppermute(sent, axis, [(i, i ^ k) for i in range(count)]).astype(F32)]
    all_to_all x2, starting transfers between devices: 6.56 us -> 9.84 us  [the longest x1 6.35 us: gather_rows(): lax.all_to_all(spread, axis, split_axis=0, concat_axis=0, tiled=True)]
    all_to_all x2, waiting for transfers between devices: 5.58 us -> 8.48 us  [the longest x1 4.83 us: per_device(): lax.all_to_all(outgoing, ('head', 'state'), split_axis=0, concat_axis=0,...]
  transfers between devices with their start and end apart: 5 -> 8, of which waited for: 4 -> 4; matrix products, arithmetic and copies ran while one was open for 3% -> 7% of each run, Pallas kernels for 0% -> 0%
where the time goes in v1:
time: 98.7 us; the launch traced here: 97.8 us
  matrix products  24.8 us (25%)
  starting transfers between devices  18.6 us (19%)
  blocking collectives  18.4 us (19%)
  waiting for transfers between devices  12.6 us (13%)
  other arithmetic  10.4 us (11%)
  local copies, waits for them, and re-layouts  10.3 us (10%)
  between operations  2.71 us (3%)
    ppermute x6, starting transfers between devices, exchange_sum(): lax.ppermute(sent, axis, [(i, i ^ k) for i in range(count)]).astype(F32)  8.78 us
    dot_general x1, matrix products, per_device(): jnp.einsum('td,ldf->ltf', row_normed, gate_proj, preferred_element_type=F32)  7.39 us
    dot_general x1, matrix products, per_device(): jnp.einsum('td,ldf->ltf', row_normed, up_proj, preferred_element_type=F32)  7.37 us
    all_gather x1, blocking collectives, per_device(): branch_all = lax.all_gather(branch_sent, 'state').astype(F32)  7.35 us
    all_to_all x1, starting transfers between devices, gather_rows(): lax.all_to_all(spread, axis, split_axis=0, concat_axis=0, tiled=True)  6.35 us
    all_gather x1, blocking collectives, per_device(): lax.all_gather(read_part.astype(BF16), 'state').astype(F32)  5.76 us
    all_gather x1, blocking collectives, per_device(): lax.all_gather(resid_cols, 'state', axis=1, tiled=True).astype(F32)  5.24 us
    all_to_all x1, waiting for transfers between devices, per_device(): lax.all_to_all(outgoing, ('head', 'state'), split_axis=0, concat_axis=0,...  4.83 us
  transfers between devices with their start and end apart: 8, of which 4 were waited for; matrix products, arithmetic and copies ran while one was open for 7% of the time, Pallas kernels for 0%

profile of v1, /device:TPU:0, one launch (start us, length us, event | category | flops | bytes accessed | tf_op | source)
XLA Modules:
  0.0 97.8 jit_solution(18436135440875717229)
XLA Ops:
  3.6 6.3 %all-to-all-start = ((bf16[4,4,640]{2,1,0:T(4,128)(2,1)}), bf16[4,4,640]{2,1,0:T(4,128)(2,1)S(1)}, u32[]{:S(2)}, u32[]{:S(2)}) async-start(bf16[4,4,640]{2,1,0:T(4,128)(2,1)} %broadcast_in_dim.27), calls=%async_computation | async-start | bytes 40960 | tf_op jit(solution)/shard_map/all_to_all | solution.py:21
  10.5 1.4 %exp.33 = f32[4,2048]{1,0:T(4,128)} exponential(f32[4,2048]{1,0:T(4,128)} %param.31) | non-fusion elementwise | bytes 65536 | tf_op jit(solution)/shard_map/exp | solution.py:111
  11.9 3.7 %all-to-all-done = bf16[4,4,640]{2,1,0:T(4,128)(2,1)S(1)} async-done(((bf16[4,4,640]{2,1,0:T(4,128)(2,1)}), bf16[4,4,640]{2,1,0:T(4,128)(2,1)S(1)}, u32[]{:S(2)}, u32[]{:S(2)}) %all-to-all-start) | async-done | bytes 20512 | tf_op jit(solution)/shard_map/all_to_all | solution.py:21
  15.9 3.0 %fusion.2 = bf16[2,16,2048]{2,1,0:T(8,128)(2,1)S(1)} fusion(bf16[2,512,2048]{2,1,0:T(8,128)(2,1)} %param.23, f32[512]{0:T(512)} %param.22, bf16[16,640]{1,0:T(8,128)(2,1)S(1)} %reshape.147), kind=kOutput, calls=%fused_computation.6 | convolution fusion | flops 67198976 | bytes 4343808 | tf_op jit(solution)/shard_map/td,kdc->ktc/dot_general | solution.py:85
  18.9 7.4 %all-gather = bf16[8,16,2176]{2,1,0:T(8,128)(2,1)S(1)} all-gather(bf16[2,16,2176]{2,1,0:T(8,128)(2,1)S(1)} %pad_maximum_fusion.1), channel_id=2, replica_groups=mesh['groups'=2,'head'=4,'state'=4] {'state'}, dimensions={0}, use_global_device_ids=true | all-gather | bytes 696320 | tf_op jit(solution)/shard_map/all_gather | solution.py:89
  27.2 1.1 %fusion.15 = f32[16,288]{1,0:T(8,128)} fusion(bf16[2048,288]{0,1:T(8,128)(2,1)S(1)} %copy-done.2, f32[16,2048]{1,0:T(8,128)S(1)} %divide_multiply_fusion), kind=kOutput, calls=%fused_computation.38 | convolution fusion | flops 18907136 | bytes 1329152 | tf_op jit(solution)/shard_map/dot_general | solution.py:99
  29.4 3.2 %collective-permute-start.2 = (f32[16,288]{1,0:T(8,128)}, f32[16,288]{1,0:T(8,128)}, u32[]{:S(2)}, u32[]{:S(2)}) collective-permute-start(f32[16,288]{1,0:T(8,128)} %fusion.15), channel_id=1, source_target_pairs={{0,12},{4,8},{8,4},{12,0},{1,13},{5,9},{9,5},{13,1},{2,14},{6,10},... | collective-permute-start | bytes 55304 | tf_op jit(solution)/shard_map/ppermute | solution.py:31
  32.6 1.4 %fusion.39 = (bf16[16,2]{1,0:T(8,128)(2,1)}, bf16[16,2]{1,0:T(8,128)(2,1)}) fusion(bf16[16,640]{1,0:T(8,128)(2,1)} %copy-done.5), kind=kLoop, calls=%fused_computation.86 | loop fusion | bytes 256 | tf_op jit(solution)/shard_map/slice | solution.py:78
  34.0 1.3 %copy.78 = bf16[16,2]{0,1:T(2,128)(2,1)} copy(bf16[16,2]{1,0:T(8,128)(2,1)} %get-tuple-element.16) | data formatting | bytes 128
  37.5 1.3 %copy.72 = f32[4,16]{1,0:T(4,128)} copy(f32[4,16]{0,1:T(8,128)} %get-tuple-element.15) | data formatting | bytes 512 | tf_op jit(solution)/shard_map/transpose | solution.py:113
  38.9 1.4 %copy.73 = f32[4,16]{1,0:T(4,128)} copy(f32[4,16]{0,1:T(8,128)} %get-tuple-element.14) | data formatting | bytes 512 | tf_op jit(solution)/shard_map/transpose | solution.py:112
  40.2 1.6 %fusion.40 = (f32[16,2048]{1,0:T(8,128)S(1)}, f32[16,2048]{1,0:T(8,128)S(1)}) fusion(f32[2048]{0:T(1024)} %param.30, bf16[256,2048]{1,0:T(8,128)(2,1)} %param.29, f32[16,288]{1,0:T(8,128)} %copy-done.6, f32[256]{0:T(256)} %param.28, f32[16]{0:T(128)} %add_rsqrt_fusion.1), kind=kOutput, calls=%fused_computation.87 | convolution fusion | flops 17051648 | bytes 1336832 | tf_op jit(solution)/shard_map/dot_general | solution.py:109
  41.8 1.8 %multiply_reduce_fusion = (bf16[16,2048]{1,0:T(8,128)(2,1)S(1)}, f32[4,16,2048]{2,1,0:T(8,128)}) fusion(f32[4,16]{1,0:T(4,128)} %copy.72, f32[16,2048]{1,0:T(8,128)S(1)} %divide_multiply_fusion, f32[4,16]{1,0:T(4,128)} %copy.73, f32[16,2048]{1,0:T(8,128)S(1)} %get-tuple-element.19, f32[4,16,2048]{2,1,0:T(8,128)S(1)} %copy-done.3, f32[4,2048]{1,0:T(4,128)} %exp.33, ...), kind=kLoop, calls=%fused_computation.18 | loop fusion | flops 884736 | bytes 1540608 | tf_op jit(solution)/shard_map/reduce_sum | solution.py:113
  43.6 5.8 %all-gather.1 = bf16[64,2048]{1,0:T(8,128)(2,1)S(1)} all-gather(bf16[16,2048]{1,0:T(8,128)(2,1)S(1)} %get-tuple-element.12), channel_id=3, replica_groups=mesh['groups'=2,'head'=4,'state'=4] {'state'}, dimensions={0}, use_global_device_ids=true | all-gather | bytes 327680 | tf_op jit(solution)/shard_map/all_gather | solution.py:114
  49.4 1.1 %convolution_convert_fusion.1 = bf16[16,512]{1,0:T(8,128)(2,1)S(1)} fusion(bf16[2048,512]{1,0:T(8,128)(2,1)S(1)} %copy-done, f32[2,16,2176]{2,1,0:T(8,128)S(1)} %convert_reduce_fusion, f32[16,2048]{1,0:T(8,128)S(1)} %convert_reduce_fusion.1, f32[16,2048]{1,0:T(8,128)S(1)} %divide_multiply_fusion, f32[16]{0:T(128)} %copy-done.9, f32[2048]{0:T(1024)} %param.32), kind=kOutput, calls=%fused_computation.10 | convolution fusion | flops 33857536 | bytes 2515008 | tf_op jit(solution)/shard_map/dot_general | solution.py:118
  50.6 3.7 %collective-permute-start.4 = (bf16[16,512]{1,0:T(8,128)(2,1)S(1)}, bf16[16,512]{1,0:T(8,128)(2,1)S(1)}, u32[]{:S(2)}, u32[]{:S(2)}) collective-permute-start(bf16[16,512]{1,0:T(8,128)(2,1)S(1)} %convolution_convert_fusion.1), channel_id=1, source_target_pairs={{0,8},{4,12},{8,0},{12,4},{1,9},{5,13},{9,1},{13,5},{2,10},{6,14},... | collective-permute-start | bytes 49160 | tf_op jit(solution)/shard_map/ppermute | solution.py:31
  56.0 3.8 %collective-permute-done.5 = bf16[16,512]{1,0:T(8,128)(2,1)S(1)} collective-permute-done((bf16[16,512]{1,0:T(8,128)(2,1)S(1)}, bf16[16,512]{1,0:T(8,128)(2,1)S(1)}, u32[]{:S(2)}, u32[]{:S(2)}) %collective-permute-start.5) | collective-permute-done | bytes 16416 | tf_op jit(solution)/shard_map/ppermute | solution.py:31
  60.5 5.2 %all_gather.16 = bf16[16,2048]{1,0:T(8,128)(2,1)S(1)} all-gather(bf16[16,512]{1,0:T(8,128)(2,1)S(1)} %fusion.20), channel_id=1, replica_groups=mesh['groups'=2,'head'=4,'state'=4] {'state'}, dimensions={1}, use_global_device_ids=true | all-gather | bytes 81920 | tf_op jit(solution)/shard_map/all_gather | solution.py:121
  65.9 1.2 %divide_reduce_fusion = (f32[8]{0:T(128)S(1)}, f32[16,8]{0,1:T(8,128)S(1)}) fusion(f32[2048,8]{0,1:T(8,128)} %param.36, bf16[16,2048]{1,0:T(8,128)(2,1)S(1)} %all_gather.16, f32[2048]{0:T(1024)} %param.35, f32[16]{0:T(128)S(1)} %add_rsqrt_fusion), kind=kOutput, calls=%fused_computation.70 | convolution fusion | flops 3211896 | bytes 139872 | tf_op jit(solution)/shard_map/dot_general | solution.py:131
  68.0 7.4 %convolution_bitcast_fusion.1 = f32[2,16,1792]{2,1,0:T(8,128)S(1)} fusion(bf16[2,2048,1792]{2,1,0:T(8,128)(2,1)} %param.39, bf16[16,2048]{1,0:T(8,128)(2,1)S(1)} %all_gather.16, f32[16]{0:T(128)S(1)} %add_rsqrt_fusion, f32[2048]{0:T(1024)} %param.35), kind=kOutput, calls=%fused_computation.2 | convolution fusion | flops 235012096 | bytes 14983232 | tf_op jit(solution)/shard_map/td,ldf->ltf/dot_general | solution.py:126
  75.5 7.4 %fusion.1 = bf16[2,16,1792]{2,1,0:T(8,128)(2,1)S(1)} fusion(bf16[2,2048,1792]{2,1,0:T(8,128)(2,1)} %param.40, f32[2,16,1792]{2,1,0:T(8,128)S(1)} %convolution_bitcast_fusion.1, bf16[16,2048]{1,0:T(8,128)(2,1)S(1)} %all_gather.16, f32[16]{0:T(128)S(1)} %add_rsqrt_fusion, f32[2048]{0:T(1024)S(1)} %copy-done.4), kind=kOutput, calls=%fused_computation.4 | convolution fusion | flops 235356160 | bytes 15097920 | tf_op jit(solution)/shard_map/td,ldf->ltf/dot_general | solution.py:127
  83.0 2.0 %fusion.3 = bf16[16,2048]{1,0:T(8,128)(2,1)S(1)} fusion(bf16[2,16,1792]{2,1,0:T(8,128)(2,1)S(1)} %fusion.1, bf16[2,1792,2048]{2,1,0:T(8,128)(2,1)S(1)} %bitcast.52, f32[2,16]{1,0:T(2,128)S(1)} %fusion.36), kind=kOutput, calls=%fused_computation.8 | convolution fusion | flops 234979328 | bytes 14860416 | tf_op jit(solution)/shard_map/ltf,lfd->ltd/dot_general | solution.py:129
  85.7 3.5 %all-to-all-start.1 = ((bf16[16,4,512]{2,1,0:T(4,128)(2,1)}), bf16[16,4,512]{2,1,0:T(4,128)(2,1)S(1)}, u32[]{:S(2)}, u32[]{:S(2)}) async-start(bf16[16,4,512]{2,1,0:T(4,128)(2,1)} %bitcast.12), calls=%async_computation.1 | async-start | bytes 131072 | tf_op jit(solution)/shard_map/all_to_all | solution.py:145
  91.2 4.8 %all-to-all-done.1 = bf16[16,4,512]{2,1,0:T(4,128)(2,1)S(1)} async-done(((bf16[16,4,512]{2,1,0:T(4,128)(2,1)}), bf16[16,4,512]{2,1,0:T(4,128)(2,1)S(1)}, u32[]{:S(2)}, u32[]{:S(2)}) %all-to-all-start.1) | async-done | bytes 65568 | tf_op jit(solution)/shard_map/all_to_all | solution.py:145
  (86 shorter events, 14.3 us)
Async XLA Ops:
  0.6 48.7 %copy-start = (bf16[2048,512]{1,0:T(8,128)(2,1)S(1)}, bf16[2048,512]{1,0:T(8,128)(2,1)}, u32[]{:S(2)}) copy-start(bf16[2048,512]{1,0:T(8,128)(2,1)} %param.34) | copy-start | bytes 6291460
  0.6 26.4 %copy-start.7 = (f32[4,2048]{1,0:T(4,128)S(1)}, f32[4,2048]{1,0:T(4,128)}, u32[]{:S(2)}) copy-start(f32[4,2048]{1,0:T(4,128)} %param.24) | copy-start | bytes 98308
  0.7 26.4 %copy-start.1 = (f32[3,16,2048]{2,1,0:T(8,128)S(1)}, f32[3,16,2048]{2,1,0:T(8,128)}, u32[]{:S(2)}) copy-start(f32[3,16,2048]{2,1,0:T(8,128)} %param.26) | copy-start | bytes 1179652
  3.6 12.0 %all-to-all-start = ((bf16[4,4,640]{2,1,0:T(4,128)(2,1)}), bf16[4,4,640]{2,1,0:T(4,128)(2,1)S(1)}, u32[]{:S(2)}, u32[]{:S(2)}) async-start(bf16[4,4,640]{2,1,0:T(4,128)(2,1)} %broadcast_in_dim.27), calls=%async_computation | async-start | bytes 40960 | tf_op jit(solution)/shard_map/all_to_all | solution.py:21
  15.6 10.7 %copy-start.5 = (bf16[16,640]{1,0:T(8,128)(2,1)}, bf16[16,640]{1,0:T(8,128)(2,1)S(1)}, u32[]{:S(2)}) copy-start(bf16[16,640]{1,0:T(8,128)(2,1)S(1)} %reshape.147) | copy-start | bytes 61444
  15.9 11.2 %copy-start.8 = (f32[2048]{0:T(1024)S(1)}, f32[2048]{0:T(1024)}, u32[]{:S(2)}) copy-start(f32[2048]{0:T(1024)} %param.25) | copy-start | bytes 24580
  15.9 11.3 %copy-start.2 = (bf16[2048,288]{0,1:T(8,128)(2,1)S(1)}, bf16[2048,288]{0,1:T(8,128)(2,1)}, u32[]{:S(2)}) copy-start(bf16[2048,288]{0,1:T(8,128)(2,1)} %param.27) | copy-start | bytes 3538948
  15.9 25.9 %copy-start.3 = (f32[4,16,2048]{2,1,0:T(8,128)S(1)}, f32[4,16,2048]{2,1,0:T(8,128)}, u32[]{:S(2)}) copy-start(f32[4,16,2048]{2,1,0:T(8,128)} %param.33) | copy-start | bytes 1572868
  28.2 7.1 %collective-permute-start = (f32[16,288]{1,0:T(8,128)}, f32[16,288]{1,0:T(8,128)}, u32[]{:S(2)}, u32[]{:S(2)}) collective-permute-start(f32[16,288]{1,0:T(8,128)} %fusion.15), channel_id=1, source_target_pairs={{0,4},{4,0},{8,12},{12,8},{1,5},{5,1},{9,13},{13,9},{2,6},{6,2},{1... | collective-permute-start | bytes 55304 | tf_op jit(solution)/shard_map/ppermute | solution.py:31
  28.9 6.5 %collective-permute-start.1 = (f32[16,288]{1,0:T(8,128)}, f32[16,288]{1,0:T(8,128)}, u32[]{:S(2)}, u32[]{:S(2)}) collective-permute-start(f32[16,288]{1,0:T(8,128)} %fusion.15), channel_id=1, source_target_pairs={{0,8},{4,12},{8,0},{12,4},{1,9},{5,13},{9,1},{13,5},{2,10},{6,14},... | collective-permute-start | bytes 55304 | tf_op jit(solution)/shard_map/ppermute | solution.py:31
  29.4 6.0 %collective-permute-start.2 = (f32[16,288]{1,0:T(8,128)}, f32[16,288]{1,0:T(8,128)}, u32[]{:S(2)}, u32[]{:S(2)}) collective-permute-start(f32[16,288]{1,0:T(8,128)} %fusion.15), channel_id=1, source_target_pairs={{0,12},{4,8},{8,4},{12,0},{1,13},{5,9},{9,5},{13,1},{2,14},{6,10},... | collective-permute-start | bytes 55304 | tf_op jit(solution)/shard_map/ppermute | solution.py:31
  36.2 0.7 copy-start.6
  40.2 14.7 %copy-start.10 = (bf16[16,2]{0,1:T(2,128)(2,1)S(1)}, bf16[16,2]{0,1:T(2,128)(2,1)}, u32[]{:S(2)}) copy-start(bf16[16,2]{0,1:T(2,128)(2,1)} %copy.78) | copy-start | bytes 196
  50.5 5.2 %collective-permute-start.3 = (bf16[16,512]{1,0:T(8,128)(2,1)S(1)}, bf16[16,512]{1,0:T(8,128)(2,1)S(1)}, u32[]{:S(2)}, u32[]{:S(2)}) collective-permute-start(bf16[16,512]{1,0:T(8,128)(2,1)S(1)} %convolution_convert_fusion.1), channel_id=1, source_target_pairs={{0,4},{4,0},{8,12},{12,8},{1,5},{5,1},{9,13},{13,9},{2,6},{6,2},{1... | collective-permute-start | bytes 49160 | tf_op jit(solution)/shard_map/ppermute | solution.py:31
  50.6 5.4 %collective-permute-start.4 = (bf16[16,512]{1,0:T(8,128)(2,1)S(1)}, bf16[16,512]{1,0:T(8,128)(2,1)S(1)}, u32[]{:S(2)}, u32[]{:S(2)}) collective-permute-start(bf16[16,512]{1,0:T(8,128)(2,1)S(1)} %convolution_convert_fusion.1), channel_id=1, source_target_pairs={{0,8},{4,12},{8,0},{12,4},{1,9},{5,13},{9,1},{13,5},{2,10},{6,14},... | collective-permute-start | bytes 49160 | tf_op jit(solution)/shard_map/ppermute | solution.py:31
  54.3 5.5 %collective-permute-start.5 = (bf16[16,512]{1,0:T(8,128)(2,1)S(1)}, bf16[16,512]{1,0:T(8,128)(2,1)S(1)}, u32[]{:S(2)}, u32[]{:S(2)}) collective-permute-start(bf16[16,512]{1,0:T(8,128)(2,1)S(1)} %convolution_convert_fusion.1), channel_id=1, source_target_pairs={{0,12},{4,8},{8,4},{12,0},{1,13},{5,9},{9,5},{13,1},{2,14},{6,10},... | collective-permute-start | bytes 49160 | tf_op jit(solution)/shard_map/ppermute | solution.py:31
  67.3 22.7 %copy-start.11 = (f32[8]{0:T(128)}, f32[8]{0:T(128)S(1)}, u32[]{:S(2)}) copy-start(f32[8]{0:T(128)S(1)} %get-tuple-element.10) | copy-start | bytes 100
  68.0 7.4 %copy-start.12 = (s32[2]{0:T(128)S(1)}, s32[2]{0:T(128)}, u32[]{:S(2)}) copy-start(s32[2]{0:T(128)} %iota_add_fusion) | copy-start | bytes 28
  68.0 7.5 %copy-start.4 = (f32[2048]{0:T(1024)S(1)}, f32[2048]{0:T(1024)}, u32[]{:S(2)}) copy-start(f32[2048]{0:T(1024)} %param.35) | copy-start | bytes 24580
  68.0 14.9 %slice-start = ((s8[14680064]{0:T(1024)(128)(4,1)}), s8[4194304]{0:T(1024)(128)(4,1)S(1)}, s32[]{:S(2)}) async-start(s8[14680064]{0:T(1024)(128)(4,1)} %bitcast.51), calls=%async_computation.2 | async-start | bytes 8388608
  68.0 14.9 %slice-start.1 = ((s8[14680064]{0:T(1024)(128)(4,1)}), s8[4194304]{0:T(1024)(128)(4,1)S(1)}, s32[]{:S(2)}) async-start(s8[14680064]{0:T(1024)(128)(4,1)} %bitcast.51), calls=%async_computation.3 | async-start | bytes 8388608
  75.5 7.4 %slice-start.2 = ((s8[14680064]{0:T(1024)(128)(4,1)}), s8[4194304]{0:T(1024)(128)(4,1)S(1)}, s32[]{:S(2)}) async-start(s8[14680064]{0:T(1024)(128)(4,1)} %bitcast.51), calls=%async_computation.4 | async-start | bytes 8388608
  75.5 7.4 %slice-start.3 = ((s8[14680064]{0:T(1024)(128)(4,1)}), s8[2097152]{0:T(1024)(128)(4,1)S(1)}, s32[]{:S(2)}) async-start(s8[14680064]{0:T(1024)(128)(4,1)} %bitcast.51), calls=%async_computation.5 | async-start | bytes 4194304
  85.7 10.4 %all-to-all-start.1 = ((bf16[16,4,512]{2,1,0:T(4,128)(2,1)}), bf16[16,4,512]{2,1,0:T(4,128)(2,1)S(1)}, u32[]{:S(2)}, u32[]{:S(2)}) async-start(bf16[16,4,512]{2,1,0:T(4,128)(2,1)} %bitcast.12), calls=%async_computation.1 | async-start | bytes 131072 | tf_op jit(solution)/shard_map/all_to_all | solution.py:145
  (1 other events, 0.5 us)

commit v2 on v1

--- a/solution.py
+++ b/solution.py
@@ -1,6 +1,10 @@
+import functools
+
 import jax
 import jax.numpy as jnp
 from jax import lax
+from jax.experimental import pallas as pl
+from jax.experimental.pallas import tpu as pltpu
 from jax.sharding import PartitionSpec as P
 
 TOPK = 2
@@ -9,17 +13,139 @@
 NORM_EPS = 1e-05
 STEP_EPS = 1e-06
 LANES = 128
+KERNEL_VMEM = 12 * 2**20
+COVER_COST = pl.CostEstimate(flops=2 * 10**10, bytes_accessed=10**8, transcendentals=0)
 BF16 = jnp.bfloat16
 F32 = jnp.float32
 
 
-def gather_rows(block, axis):
+def in_vmem(array):
+    return pltpu.with_memory_space_constraint(array, pltpu.VMEM)
+
+
+def pack_kernel(tok_ref, ids_ref, slot_ref, out_ref):
+    copies, rows, _ = out_ref.shape
+    cols = tok_ref.shape[1]
+    lane = lax.broadcasted_iota(jnp.int32, (rows, LANES), 1)
+    routing = jnp.zeros((rows, LANES), jnp.int32)
+    for k in range(TOPK):
+        routing = jnp.where(lane == k, ids_ref[:, k : k + 1], routing)
+        slot = jnp.minimum(slot_ref[:, k : k + 1], CAP)
+        routing = jnp.where(lane == TOPK + k, slot, routing)
+    routing = routing.astype(F32).astype(BF16)
+    for c in range(copies):
+        out_ref[c, :, :cols] = tok_ref[...]
+        out_ref[c, :, cols:] = routing
+
+
+def gather_tokens(tokens, expert_ids, slot_ids, axis):
     count = lax.axis_size(axis)
-    if count > 8:
-        return lax.all_gather(block, axis, axis=0, tiled=True)
-    spread = jnp.broadcast_to(block[None], (count, *block.shape))
+    rows, cols = tokens.shape
+    direct = count > 8
+    spread = pl.pallas_call(
+        pack_kernel,
+        out_shape=jax.ShapeDtypeStruct((1 if direct else count, rows, cols + LANES), BF16),
+        compiler_params=pltpu.CompilerParams(vmem_limit_bytes=KERNEL_VMEM),
+        cost_estimate=COVER_COST,
+        name="pack",
+    )(tokens, expert_ids, slot_ids)
+    if direct:
+        return lax.all_gather(spread[0], axis, axis=0, tiled=True)
     spread = lax.all_to_all(spread, axis, split_axis=0, concat_axis=0, tiled=True)
-    return spread.reshape(count * block.shape[0], *block.shape[1:])
+    return spread.reshape(count * rows, cols + LANES)
+
+
+def state_kernel(
+    index_ref, proj_ref, *refs, n_parts, dt_rank, d_state
+):
+    part_refs = refs[: n_parts - 1]
+    (gain_ref, step_ref, bias_ref, decay_ref, ssm_ref, conv_ref, new_ref, read_ref) = refs[
+        n_parts - 1 :
+    ]
+    projected = proj_ref[...]
+    if n_parts == 4:
+        projected = (projected + part_refs[0][...]) + (part_refs[1][...] + part_refs[2][...])
+    low = projected[:, :dt_rank]
+    vectors = projected[:, dt_rank:]
+    inv = lax.rsqrt(jnp.mean(low * low, axis=1, keepdims=True) + STEP_EPS)
+    step_normed = (low * inv * gain_ref[...]).astype(BF16)
+    slab, rows, channels = ssm_ref.shape
+    first = index_ref[0] * slab
+    lane = lax.broadcasted_iota(jnp.int32, vectors.shape, 1)
+
+    def column(at):
+        return jnp.sum(jnp.where(lane == at, vectors, 0.0), axis=1, keepdims=True)
+
+    b_cols = [column(first + n) for n in range(slab)]
+    c_cols = [column(d_state + first + n) for n in range(slab)]
+    chunk = min(channels, 256)
+    for at in range(0, channels, chunk):
+        span = slice(at, at + chunk)
+        pre = jnp.dot(step_normed, step_ref[:, span], preferred_element_type=F32)
+        pre = pre + bias_ref[:, span]
+        step = jnp.maximum(pre, 0.0) + jnp.log1p(jnp.exp(-jnp.abs(pre)))
+        rate = jnp.exp(decay_ref[:, span])
+        step_conv = step * conv_ref[:, span]
+        read = jnp.zeros((rows, chunk), F32)
+        for n in range(slab):
+            fresh = jnp.exp(-step * rate[n : n + 1]) * ssm_ref[n, :, span] + b_cols[n] * step_conv
+            new_ref[n, :, span] = fresh
+            read = read + c_cols[n] * fresh
+        read_ref[:, span] = read.astype(BF16)
+
+
+def experts_kernel(
+    own_ref, resid_ref, route_ref, norm_ref, router_ref, gate_ref, up_ref, down_ref,
+    out_ref, logit_ref, acc_ref, hidden_ref, held_ref, sems,
+):
+    local, _, hidden_units = gate_ref.shape
+    chunk = 256 if hidden_units % 256 == 0 else hidden_units
+    copies = []
+    for e in range(local):
+        copies.append(pltpu.make_async_copy(down_ref.at[e], held_ref.at[e], sems.at[e]))
+        copies[e].start()
+    blocks, own_rows, own_cols = out_ref.shape
+    rows, width = resid_ref.shape
+    states = width // own_cols
+    resid = resid_ref[...].astype(F32)
+    inv = lax.rsqrt(jnp.mean(resid * resid, axis=1, keepdims=True) + NORM_EPS)
+    scaled = resid * norm_ref[...]
+    logits = inv * jnp.dot(
+        scaled, router_ref[...], precision=lax.Precision.HIGHEST, preferred_element_type=F32
+    )
+    logit_ref[...] = logits
+    row_normed = (scaled * inv).astype(BF16)
+    route = route_ref[...].astype(F32)
+    lane = lax.broadcasted_iota(jnp.int32, logits.shape, 1)
+    picks = [route[:, k : k + 1].astype(jnp.int32) for k in range(TOPK)]
+    kept = [route[:, TOPK + k : TOPK + k + 1] < CAP for k in range(TOPK)]
+    chosen = [jnp.sum(jnp.where(lane == p, logits, 0.0), axis=1, keepdims=True) for p in picks]
+    mix = [
+        jnp.where(kept[k], jax.nn.sigmoid(chosen[k] - chosen[1 - k]), 0.0) for k in range(TOPK)
+    ]
+    for e in range(local):
+        for at in range(0, hidden_units, chunk):
+            span = slice(at, at + chunk)
+            gate = jnp.dot(row_normed, gate_ref[e, :, span], preferred_element_type=F32)
+            up = jnp.dot(row_normed, up_ref[e, :, span], preferred_element_type=F32)
+            hidden_ref[e, :, span] = (gate / (1.0 + jnp.exp(-gate)) * up).astype(BF16)
+    for e in range(local):
+        weight = jnp.zeros((rows, 1), F32)
+        for k in range(TOPK):
+            weight = weight + jnp.where(picks[k] == own_ref[e], mix[k], 0.0)
+        copies[e].wait()
+        for at in range(0, width, 512):
+            span = slice(at, at + 512)
+            value = weight * jnp.dot(
+                hidden_ref[e], held_ref[e, :, span], preferred_element_type=F32
+            )
+            if e == 0:
+                acc_ref[:, span] = value
+            else:
+                acc_ref[:, span] += value
+    for b in range(blocks):
+        at, col = (b // states) * own_rows, (b % states) * own_cols
+        out_ref[b] = acc_ref[at : at + own_rows, col : col + own_cols].astype(BF16)
 
 
 def exchange_sum(part, axis, dtype):
@@ -32,6 +158,15 @@
         for k in range(1, count)
     ]
     return (sent.astype(F32) + others[0]) + (others[1] + others[2])
+
+
+def exchange_parts(part, axis):
+    count = lax.axis_size(axis)
+    if count != 4:
+        return (lax.psum(part, axis),)
+    return (part,) + tuple(
+        lax.ppermute(part, axis, [(i, i ^ k) for i in range(count)]) for k in range(1, count)
+    )
 
 
 def per_device(
@@ -69,9 +204,7 @@
     d_state = state_slab * state_count
     channels = conv_bias.shape[0]
 
-    routing = jnp.concatenate([expert_ids, jnp.minimum(slot_ids, CAP)], axis=1).astype(BF16)
-    routing = jnp.pad(routing, ((0, 0), (0, LANES - 2 * TOPK)))
-    packed = gather_rows(jnp.concatenate([tokens, routing], axis=1), "head")
+    packed = gather_tokens(tokens, expert_ids, slot_ids, "head")
     tok_all = packed[:, :own_cols]
     rows = tok_all.shape[0]
     expert_all = packed[:, own_cols : own_cols + TOPK].astype(jnp.int32)
@@ -97,51 +230,67 @@
     new_conv = window[1:]
 
     proj_part = jnp.dot(conv_out.astype(BF16), state_proj, preferred_element_type=F32)
-    projected = exchange_sum(proj_part, "head", F32)
-    step_low = projected[:, :dt_rank]
-    b_input = lax.dynamic_slice_in_dim(projected, dt_rank + state_index * state_slab, state_slab, 1)
-    c_output = lax.dynamic_slice_in_dim(
-        projected, dt_rank + d_state + state_index * state_slab, state_slab, 1
-    )
-    step_inv = lax.rsqrt(jnp.mean(step_low * step_low, axis=1, keepdims=True) + STEP_EPS)
-    step_normed = (step_low * step_inv * step_gain).astype(BF16)
-    step_size = jax.nn.softplus(
-        jnp.dot(step_normed, step_proj, preferred_element_type=F32) + step_bias
-    )
-    decay_rate = jnp.exp(-step_size[None] * jnp.exp(decay_log)[:, None, :])
-    new_state = decay_rate * ssm_state + step_size[None] * b_input.T[:, :, None] * conv_out[None]
-    read_part = jnp.sum(c_output.T[:, :, None] * new_state, axis=0)
-    readout = jnp.sum(lax.all_gather(read_part.astype(BF16), "state").astype(F32), axis=0)
+    parts = exchange_parts(proj_part, "head")
+    vmem = pl.BlockSpec(memory_space=pltpu.VMEM)
+    smem = pl.BlockSpec(memory_space=pltpu.SMEM)
+    new_state, read_part = pl.pallas_call(
+        functools.partial(
+            state_kernel, n_parts=len(parts), dt_rank=dt_rank, d_state=d_state
+        ),
+        in_specs=[smem] + [vmem] * (len(parts) + 6),
+        out_shape=(
+            jax.ShapeDtypeStruct(ssm_state.shape, F32),
+            jax.ShapeDtypeStruct((rows, channels), BF16),
+        ),
+        compiler_params=pltpu.CompilerParams(vmem_limit_bytes=KERNEL_VMEM),
+        cost_estimate=COVER_COST,
+        name="state_step",
+    )(
+        state_index.reshape(1),
+        *parts,
+        step_gain[None],
+        in_vmem(step_proj),
+        step_bias[None],
+        decay_log,
+        in_vmem(ssm_state),
+        conv_out,
+    )
+    readout = jnp.sum(lax.all_gather(read_part, "state").astype(F32), axis=0)
     mixer_act = ((readout + skip_gain * conv_out) * jax.nn.silu(gate_branch)).astype(BF16)
 
     mixer_sum = exchange_sum(
         jnp.dot(mixer_act, output_proj, preferred_element_type=F32), "head", BF16
     )
     resid_cols = (tok_f32 + mixer_sum).astype(BF16)
-    resid_all = lax.all_gather(resid_cols, "state", axis=1, tiled=True).astype(F32)
-    inv_second = lax.rsqrt(jnp.mean(resid_all * resid_all, axis=1, keepdims=True) + NORM_EPS)
-    scaled = resid_all * moe_norm
-    row_normed = (scaled * inv_second).astype(BF16)
-
-    gate_val = jnp.einsum("td,ldf->ltf", row_normed, gate_proj, preferred_element_type=F32)
-    up_val = jnp.einsum("td,ldf->ltf", row_normed, up_proj, preferred_element_type=F32)
-    hidden = (jax.nn.silu(gate_val) * up_val).astype(BF16)
-    value = jnp.einsum("ltf,lfd->ltd", hidden, down_proj, preferred_element_type=F32)
-
-    logits = inv_second * jnp.dot(scaled, router_weight, precision=lax.Precision.HIGHEST)
-    expert_hit = expert_all[:, :, None] == jnp.arange(experts, dtype=jnp.int32)[None, None, :]
-    chosen = jnp.sum(jnp.where(expert_hit, logits[:, None, :], 0.0), axis=2)
-    gate_probs = jax.nn.sigmoid(chosen - chosen[:, ::-1])
-    mix_weight = jnp.where(kept_all, gate_probs, 0.0)
+    resid_all = lax.all_gather(resid_cols, "state", axis=1, tiled=True)
     local_experts = gate_proj.shape[0]
     split = head_count * local_experts // experts
     own_experts = (head_index * local_experts + jnp.arange(local_experts, dtype=jnp.int32)) // split
-    own_hit = expert_all[None, :, :] == own_experts[:, None, None]
-    own_weight = jnp.sum(jnp.where(own_hit, mix_weight[None], 0.0), axis=2)
-    mix_part = jnp.sum(own_weight[:, :, None] * value, axis=0).astype(BF16)
-
-    outgoing = mix_part.reshape(head_count, own_rows, state_count, own_cols)
-    outgoing = outgoing.transpose(0, 2, 1, 3).reshape(head_count * state_count, own_rows, own_cols)
+    outgoing, logits = pl.pallas_call(
+        experts_kernel,
+        in_specs=[smem] + [vmem] * 6 + [pl.BlockSpec(memory_space=pltpu.HBM)],
+        out_shape=(
+            jax.ShapeDtypeStruct((head_count * state_count, own_rows, own_cols), BF16),
+            jax.ShapeDtypeStruct((rows, experts), F32),
+        ),
+        scratch_shapes=[
+            pltpu.VMEM((rows, model_width), F32),
+            pltpu.VMEM((local_experts, rows, gate_proj.shape[2]), BF16),
+            pltpu.VMEM(down_proj.shape, BF16),
+            pltpu.SemaphoreType.DMA((local_experts,)),
+        ],
+        compiler_params=pltpu.CompilerParams(vmem_limit_bytes=2 * KERNEL_VMEM),
+        name="experts",
+    )(
+        own_experts,
+        resid_all,
+        packed[:, own_cols:],
+        moe_norm[None],
+        router_weight,
+        in_vmem(gate_proj),
+        in_vmem(up_proj),
+        down_proj,
+    )
     returned = lax.all_to_all(
         outgoing, ("head", "state"), split_axis=0, concat_axis=0, tiled=True
     )
@@ -149,6 +298,7 @@
     resid_own = lax.dynamic_slice_in_dim(resid_cols, head_index * own_rows, own_rows, 0)
     layer_out = (resid_own.astype(F32) + expert_mix).astype(BF16)
 
+    expert_hit = expert_all[:, :, None] == jnp.arange(experts, dtype=jnp.int32)[None, None, :]
     load_sum = jnp.sum(jnp.where(expert_hit & kept_all[:, :, None], 1.0, 0.0), axis=(0, 1)).astype(
         F32
     )

time: 98.7 us -> 85.1 us (0.86)
  matrix products: 24.8 us -> 4.62 us
  Pallas kernels: 0 us -> 13.6 us
  other arithmetic: 10.4 us -> 2.91 us
  waiting for transfers between devices: 12.6 us -> 17 us
  local copies, waits for them, and re-layouts: 10.3 us -> 6.49 us
    dot_general x5 -> x0, matrix products: 19.6 us -> none  [the longest x1 7.39 us: per_device(): jnp.einsum('td,ldf->ltf', row_normed, gate_proj, preferred_element_type=F32)]
    pallas_call x0 -> x3, Pallas kernels: none -> 13.6 us  [the longest x1 11.7 us: per_device(): pl.pallas_call(experts_kernel, in_specs=[smem] + [vmem] * 6 + [pl.BlockSp...]
    ppermute x0 -> x3, starting transfers between devices: none -> 4.42 us  [exchange_parts(): lax.ppermute(part, axis, [(i, i ^ k) for i in range(count)])]
    ppermute x6 -> x3, starting transfers between devices: 8.78 us -> 4.4 us  [exchange_sum(): lax.ppermute(sent, axis, [(i, i ^ k) for i in range(count)]).astype(F32)]
    transpose x4 -> x0, local copies, waits for them, and re-layouts: 4.02 us -> none  [the longest x2 2.02 us: per_device(): b_input.T[:, :, None]]
    unnamed x38 -> x54, local copies, waits for them, and re-layouts: 2.8 us -> 6.29 us
    reduce_sum x5 -> x2, other arithmetic: 2.14 us -> 0.06 us  [the longest x1 0.03 us: per_device(): readout = jnp.sum(lax.all_gather(read_part, 'state').astype(F32), axis=0)]
    all_to_all x1, waiting for transfers between devices: 3.65 us -> 5.28 us  [gather_tokens(): lax.all_to_all(spread, axis, split_axis=0, concat_axis=0, tiled=True)]
  transfers between devices with their start and end apart: 8 -> 8, of which waited for: 4 -> 6; matrix products, arithmetic and copies ran while one was open for 7% -> 2% of each run, Pallas kernels for 0% -> 0%
where the time goes in v2:
time: 85.1 us; the launch traced here: 84.7 us
  starting transfers between devices  18.7 us (22%)
  blocking collectives  18.6 us (22%)
  waiting for transfers between devices  17 us (20%)
  Pallas kernels  13.6 us (16%)
  local copies, waits for them, and re-layouts  6.49 us (8%)
  matrix products  4.62 us (5%)
  other arithmetic  2.91 us (3%)
  between operations  2.72 us (3%)
    pallas_call x1, Pallas kernels, per_device(): pl.pallas_call(experts_kernel, in_specs=[smem] + [vmem] * 6 + [pl.BlockSp...  11.7 us
    all_gather x1, blocking collectives, per_device(): branch_all = lax.all_gather(branch_sent, 'state').astype(F32)  7.48 us
    all_to_all x1, starting transfers between devices, gather_tokens(): lax.all_to_all(spread, axis, split_axis=0, concat_axis=0, tiled=True)  6.35 us
    unnamed x54, local copies, waits for them, and re-layouts  6.29 us
    all_gather x1, blocking collectives, per_device(): readout = jnp.sum(lax.all_gather(read_part, 'state').astype(F32), axis=0)  5.89 us
    all_to_all x1, waiting for transfers between devices, per_device(): lax.all_to_all(outgoing, ('head', 'state'), split_axis=0, concat_axis=0,...  5.57 us
    all_to_all x1, waiting for transfers between devices, gather_tokens(): lax.all_to_all(spread, axis, split_axis=0, concat_axis=0, tiled=True)  5.28 us
    all_gather x1, blocking collectives, per_device(): resid_all = lax.all_gather(resid_cols, 'state', axis=1, tiled=True)  5.24 us
  transfers between devices with their start and end apart: 8, of which 6 were waited for; matrix products, arithmetic and copies ran while one was open for 2% of the time, Pallas kernels for 0%

profile of v2, /device:TPU:0, one launch (start us, length us, event | category | flops | bytes accessed | tf_op | source)
XLA Modules:
  0.0 84.7 jit_solution(10150547978401638123)
XLA Ops:
  0.6 0.9 %copy.44.ids_ref = s32[4,2]{1,0:T(4,128)S(1)} copy(s32[4,2]{0,1:T(2,128)} %param.37) | data formatting | bytes 64 | tf_op args[16]
  1.6 0.8 copy.45.slot_ref
  2.3 0.7 copy-done.6
  3.0 0.7 pack.1
  3.7 6.3 %all-to-all-start = ((bf16[4,4,640]{2,1,0:T(4,128)(2,1)}), bf16[4,4,640]{2,1,0:T(4,128)(2,1)S(1)}, u32[]{:S(2)}, u32[]{:S(2)}) async-start(bf16[4,4,640]{2,1,0:T(4,128)(2,1)} %pack.1), calls=%async_computation | async-start | bytes 40960 | tf_op jit(solution)/shard_map/all_to_all | solution.py:54
  10.4 5.3 %all-to-all-done = bf16[4,4,640]{2,1,0:T(4,128)(2,1)S(1)} async-done(((bf16[4,4,640]{2,1,0:T(4,128)(2,1)}), bf16[4,4,640]{2,1,0:T(4,128)(2,1)S(1)}, u32[]{:S(2)}, u32[]{:S(2)}) %all-to-all-start) | async-done | bytes 20512 | tf_op jit(solution)/shard_map/all_to_all | solution.py:54
  15.9 2.8 %fusion = bf16[2,16,2048]{2,1,0:T(8,128)(2,1)S(1)} fusion(bf16[2,512,2048]{2,1,0:T(8,128)(2,1)} %param.23, f32[512]{0:T(512)S(1)} %copy-done.15, bf16[16,640]{1,0:T(8,128)(2,1)S(1)} %reshape.81), kind=kOutput, calls=%fused_computation.1 | convolution fusion | flops 67198976 | bytes 4343808 | tf_op jit(solution)/shard_map/td,kdc->ktc/dot_general | solution.py:218
  18.9 7.5 %all-gather = bf16[8,16,2176]{2,1,0:T(8,128)(2,1)S(1)} all-gather(bf16[2,16,2176]{2,1,0:T(8,128)(2,1)S(1)} %pad_maximum_fusion.1), channel_id=2, replica_groups=mesh['groups'=2,'head'=4,'state'=4] {'state'}, dimensions={0}, use_global_device_ids=true | all-gather | bytes 696320 | tf_op jit(solution)/shard_map/all_gather | solution.py:222
  27.6 0.7 collective-permute-start
  28.8 3.2 %collective-permute-start.2 = (f32[16,288]{1,0:T(8,128)S(1)}, f32[16,288]{1,0:T(8,128)S(1)}, u32[]{:S(2)}, u32[]{:S(2)}) collective-permute-start(f32[16,288]{1,0:T(8,128)S(1)} %fusion.7.proj_ref), channel_id=1, source_target_pairs={{0,12},{4,8},{8,4},{12,0},{1,13},{5,9},{9,5},{13,1},{2,14},{6,10},... | collective-permute-start | bytes 55304 | tf_op jit(solution)/shard_map/ppermute | solution.py:168
  32.0 0.8 fusion.3
  33.5 1.0 %collective-permute-done.2.refs_2_ = f32[16,288]{1,0:T(8,128)S(1)} collective-permute-done((f32[16,288]{1,0:T(8,128)S(1)}, f32[16,288]{1,0:T(8,128)S(1)}, u32[]{:S(2)}, u32[]{:S(2)}) %collective-permute-start.2) | collective-permute-done | bytes 18464 | tf_op jit(solution)/shard_map/ppermute | solution.py:168
  34.5 1.4 %copy-done.2 = bf16[256,2048]{1,0:T(8,128)(2,1)S(1)} copy-done((bf16[256,2048]{1,0:T(8,128)(2,1)S(1)}, bf16[256,2048]{1,0:T(8,128)(2,1)}, u32[]{:S(2)}) %copy-start.2) | copy-done | bytes 1048600
  35.9 1.7 %copy-done.3 = f32[4,16,2048]{2,1,0:T(8,128)S(1)} copy-done((f32[4,16,2048]{2,1,0:T(8,128)S(1)}, f32[4,16,2048]{2,1,0:T(8,128)}, u32[]{:S(2)}) %copy-start.3) | copy-done | bytes 524312
  37.6 1.3 %state_step.1 = (f32[4,16,2048]{2,1,0:T(8,128)}, bf16[16,2048]{1,0:T(8,128)(2,1)S(1)}) custom-call(s32[1]{0:T(128)} %bitcast.index_ref, f32[16,288]{1,0:T(8,128)S(1)} %fusion.7.proj_ref, f32[16,288]{1,0:T(8,128)S(1)} %collective-permute-done.refs_0_, f32[16,288]{1,0:T(8,128)S(1)} %collective-permute-done.1.refs_1_, ...), custom_call_target="tpu_custom_call" | custom-call | flops 20000000000 | bytes 100000000 | tf_op jit(solution)/shard_map/state_step/pallas_call | solution.py:236
  38.9 5.9 %all-gather.1 = bf16[64,2048]{1,0:T(8,128)(2,1)S(1)} all-gather(bf16[16,2048]{1,0:T(8,128)(2,1)S(1)} %get-tuple-element.9), channel_id=3, replica_groups=mesh['groups'=2,'head'=4,'state'=4] {'state'}, dimensions={0}, use_global_device_ids=true | all-gather | bytes 327680 | tf_op jit(solution)/shard_map/all_gather | solution.py:258
  44.8 1.3 %convolution_convert_fusion.1 = bf16[16,512]{1,0:T(8,128)(2,1)S(1)} fusion(bf16[2048,512]{1,0:T(8,128)(2,1)S(1)} %copy-done, f32[2,16,2176]{2,1,0:T(8,128)} %copy-done.10, f32[16,2048]{1,0:T(8,128)S(1)} %convert_reduce_fusion.1, f32[16,2048]{1,0:T(8,128)S(1)} %divide_multiply_fusion.refs_8_, f32[16]{0:T(128)S(1)} %fusion.20, f32[2048]{0:T(1024)S(1)} %copy-done.13), kind=kOutput, calls=%fused_computation.3 | convolution fusion | flops 33857536 | bytes 2515008 | tf_op jit(solution)/shard_map/dot_general | solution.py:262
  46.3 3.7 %collective-permute-start.4 = (bf16[16,512]{1,0:T(8,128)(2,1)S(1)}, bf16[16,512]{1,0:T(8,128)(2,1)S(1)}, u32[]{:S(2)}, u32[]{:S(2)}) collective-permute-start(bf16[16,512]{1,0:T(8,128)(2,1)S(1)} %convolution_convert_fusion.1), channel_id=1, source_target_pairs={{0,8},{4,12},{8,0},{12,4},{1,9},{5,13},{9,1},{13,5},{2,10},{6,14},... | collective-permute-start | bytes 49160 | tf_op jit(solution)/shard_map/ppermute | solution.py:157
  50.7 1.0 %collective-permute-done.4 = bf16[16,512]{1,0:T(8,128)(2,1)S(1)} collective-permute-done((bf16[16,512]{1,0:T(8,128)(2,1)S(1)}, bf16[16,512]{1,0:T(8,128)(2,1)S(1)}, u32[]{:S(2)}, u32[]{:S(2)}) %collective-permute-start.4) | collective-permute-done | bytes 16416 | tf_op jit(solution)/shard_map/ppermute | solution.py:157
  51.6 3.8 %collective-permute-done.5 = bf16[16,512]{1,0:T(8,128)(2,1)S(1)} collective-permute-done((bf16[16,512]{1,0:T(8,128)(2,1)S(1)}, bf16[16,512]{1,0:T(8,128)(2,1)S(1)}, u32[]{:S(2)}, u32[]{:S(2)}) %collective-permute-start.5) | collective-permute-done | bytes 16416 | tf_op jit(solution)/shard_map/ppermute | solution.py:157
  55.5 5.2 %all_gather.19.resid_ref = bf16[16,2048]{1,0:T(8,128)(2,1)S(1)} all-gather(bf16[16,512]{1,0:T(8,128)(2,1)S(1)} %fusion.12), channel_id=1, replica_groups=mesh['groups'=2,'head'=4,'state'=4] {'state'}, dimensions={1}, use_global_device_ids=true | all-gather | bytes 81920 | tf_op jit(solution)/shard_map/all_gather | solution.py:265
  60.8 11.7 %experts.1 = (bf16[16,4,512]{2,1,0:T(4,128)(2,1)}, f32[16,8]{1,0:T(8,128)S(1)}) custom-call(s32[2]{0:T(128)S(1)} %iota_add_fusion.own_ref, bf16[16,2048]{1,0:T(8,128)(2,1)S(1)} %all_gather.19.resid_ref, bf16[16,128]{1,0:T(8,128)(2,1)S(1)} %slice.41.route_ref, f32[1,2048]{1,0:T(1,128)S(1)} %bitcast.35, f32[2048,8]{1,0:T(8,128)S(1)} %copy.47.router_ref, ...), custom_call_target="tpu_custom_call" | custom-call | tf_op jit(solution)/shard_map/experts/pallas_call | solution.py:269
  72.5 3.5 %all-to-all-start.1 = ((bf16[16,4,512]{2,1,0:T(4,128)(2,1)}), bf16[16,4,512]{2,1,0:T(4,128)(2,1)S(1)}, u32[]{:S(2)}, u32[]{:S(2)}) async-start(bf16[16,4,512]{2,1,0:T(4,128)(2,1)} %get-tuple-element.10), calls=%async_computation.1 | async-start | bytes 131072 | tf_op jit(solution)/shard_map/all_to_all | solution.py:294
  77.3 5.6 %all-to-all-done.1 = bf16[16,4,512]{2,1,0:T(4,128)(2,1)S(1)} async-done(((bf16[16,4,512]{2,1,0:T(4,128)(2,1)}), bf16[16,4,512]{2,1,0:T(4,128)(2,1)S(1)}, u32[]{:S(2)}, u32[]{:S(2)}) %all-to-all-start.1) | async-done | bytes 65568 | tf_op jit(solution)/shard_map/all_to_all | solution.py:294
  (84 shorter events, 5.3 us)
Async XLA Ops:
  0.6 44.2 %copy-start = (bf16[2048,512]{1,0:T(8,128)(2,1)S(1)}, bf16[2048,512]{1,0:T(8,128)(2,1)}, u32[]{:S(2)}) copy-start(bf16[2048,512]{1,0:T(8,128)(2,1)} %param.34) | copy-start | bytes 6291460
  3.0 12.9 %copy-start.15 = (f32[512]{0:T(512)S(1)}, f32[512]{0:T(512)}, u32[]{:S(2)}) copy-start(f32[512]{0:T(512)} %param.22) | copy-start | bytes 6148
  3.7 12.0 %all-to-all-start = ((bf16[4,4,640]{2,1,0:T(4,128)(2,1)}), bf16[4,4,640]{2,1,0:T(4,128)(2,1)S(1)}, u32[]{:S(2)}, u32[]{:S(2)}) async-start(bf16[4,4,640]{2,1,0:T(4,128)(2,1)} %pack.1), calls=%async_computation | async-start | bytes 40960 | tf_op jit(solution)/shard_map/all_to_all | solution.py:54
  18.8 8.3 %copy-start.14 = (f32[2048]{0:T(1024)S(1)}, f32[2048]{0:T(1024)}, u32[]{:S(2)}) copy-start(f32[2048]{0:T(1024)} %param.25) | copy-start | bytes 24580
  18.8 8.4 %copy-start.9 = (bf16[2048,288]{0,1:T(8,128)(2,1)S(1)}, bf16[2048,288]{0,1:T(8,128)(2,1)}, u32[]{:S(2)}) copy-start(bf16[2048,288]{0,1:T(8,128)(2,1)} %param.27) | copy-start | bytes 3538948
  26.3 8.1 %copy-start.5 = (f32[2048]{0:T(1024)S(1)}, f32[2048]{0:T(1024)}, u32[]{:S(2)}) copy-start(f32[2048]{0:T(1024)} %param.30) | copy-start | bytes 24580
  26.3 8.1 %copy-start.7 = (f32[256]{0:T(256)S(1)}, f32[256]{0:T(256)}, u32[]{:S(2)}) copy-start(f32[256]{0:T(256)} %param.28) | copy-start | bytes 3076
  27.6 5.4 %collective-permute-start = (f32[16,288]{1,0:T(8,128)S(1)}, f32[16,288]{1,0:T(8,128)S(1)}, u32[]{:S(2)}, u32[]{:S(2)}) collective-permute-start(f32[16,288]{1,0:T(8,128)S(1)} %fusion.7.proj_ref), channel_id=1, source_target_pairs={{0,4},{4,0},{8,12},{12,8},{1,5},{5,1},{9,13},{13,9},{2,6},{6,2},{1... | collective-permute-start | bytes 55304 | tf_op jit(solution)/shard_map/ppermute | solution.py:168
  28.3 5.1 %collective-permute-start.1 = (f32[16,288]{1,0:T(8,128)S(1)}, f32[16,288]{1,0:T(8,128)S(1)}, u32[]{:S(2)}, u32[]{:S(2)}) collective-permute-start(f32[16,288]{1,0:T(8,128)S(1)} %fusion.7.proj_ref), channel_id=1, source_target_pairs={{0,8},{4,12},{8,0},{12,4},{1,9},{5,13},{9,1},{13,5},{2,10},{6,14},... | collective-permute-start | bytes 55304 | tf_op jit(solution)/shard_map/ppermute | solution.py:168
  28.8 5.6 %collective-permute-start.2 = (f32[16,288]{1,0:T(8,128)S(1)}, f32[16,288]{1,0:T(8,128)S(1)}, u32[]{:S(2)}, u32[]{:S(2)}) collective-permute-start(f32[16,288]{1,0:T(8,128)S(1)} %fusion.7.proj_ref), channel_id=1, source_target_pairs={{0,12},{4,8},{8,4},{12,0},{1,13},{5,9},{9,5},{13,1},{2,14},{6,10},... | collective-permute-start | bytes 55304 | tf_op jit(solution)/shard_map/ppermute | solution.py:168
  34.5 26.3 %slice-start = ((s8[14680064]{0:T(1024)(128)(4,1)}), s8[4194304]{0:T(1024)(128)(4,1)S(1)}, s32[]{:S(2)}) async-start(s8[14680064]{0:T(1024)(128)(4,1)} %bitcast.31), calls=%async_computation.2 | async-start | bytes 8388608
  34.5 26.3 %slice-start.4 = ((s8[14680064]{0:T(1024)(128)(4,1)}), s8[4194304]{0:T(1024)(128)(4,1)S(1)}, s32[]{:S(2)}) async-start(s8[14680064]{0:T(1024)(128)(4,1)} %bitcast.33), calls=%async_computation.6 | async-start | bytes 8388608
  37.6 23.2 %slice-start.1 = ((s8[14680064]{0:T(1024)(128)(4,1)}), s8[4194304]{0:T(1024)(128)(4,1)S(1)}, s32[]{:S(2)}) async-start(s8[14680064]{0:T(1024)(128)(4,1)} %bitcast.31), calls=%async_computation.3 | async-start | bytes 8388608
  37.6 23.2 %slice-start.2 = ((s8[14680064]{0:T(1024)(128)(4,1)}), s8[4194304]{0:T(1024)(128)(4,1)S(1)}, s32[]{:S(2)}) async-start(s8[14680064]{0:T(1024)(128)(4,1)} %bitcast.31), calls=%async_computation.4 | async-start | bytes 8388608
  37.6 23.2 %slice-start.3 = ((s8[14680064]{0:T(1024)(128)(4,1)}), s8[2097152]{0:T(1024)(128)(4,1)S(1)}, s32[]{:S(2)}) async-start(s8[14680064]{0:T(1024)(128)(4,1)} %bitcast.31), calls=%async_computation.5 | async-start | bytes 4194304
  37.6 23.2 %slice-start.5 = ((s8[14680064]{0:T(1024)(128)(4,1)}), s8[4194304]{0:T(1024)(128)(4,1)S(1)}, s32[]{:S(2)}) async-start(s8[14680064]{0:T(1024)(128)(4,1)} %bitcast.33), calls=%async_computation.7 | async-start | bytes 8388608
  37.6 23.2 %slice-start.6 = ((s8[14680064]{0:T(1024)(128)(4,1)}), s8[4194304]{0:T(1024)(128)(4,1)S(1)}, s32[]{:S(2)}) async-start(s8[14680064]{0:T(1024)(128)(4,1)} %bitcast.33), calls=%async_computation.8 | async-start | bytes 8388608
  37.6 23.2 %slice-start.7 = ((s8[14680064]{0:T(1024)(128)(4,1)}), s8[2097152]{0:T(1024)(128)(4,1)S(1)}, s32[]{:S(2)}) async-start(s8[14680064]{0:T(1024)(128)(4,1)} %bitcast.33), calls=%async_computation.9 | async-start | bytes 4194304
  38.9 21.9 %copy-start.1 = (f32[2048]{0:T(1024)S(1)}, f32[2048]{0:T(1024)}, u32[]{:S(2)}) copy-start(f32[2048]{0:T(1024)} %param.35) | copy-start | bytes 24580
  46.2 4.5 %collective-permute-start.3 = (bf16[16,512]{1,0:T(8,128)(2,1)S(1)}, bf16[16,512]{1,0:T(8,128)(2,1)S(1)}, u32[]{:S(2)}, u32[]{:S(2)}) collective-permute-start(bf16[16,512]{1,0:T(8,128)(2,1)S(1)} %convolution_convert_fusion.1), channel_id=1, source_target_pairs={{0,4},{4,0},{8,12},{12,8},{1,5},{5,1},{9,13},{13,9},{2,6},{6,2},{1... | collective-permute-start | bytes 49160 | tf_op jit(solution)/shard_map/ppermute | solution.py:157
  46.3 5.4 %collective-permute-start.4 = (bf16[16,512]{1,0:T(8,128)(2,1)S(1)}, bf16[16,512]{1,0:T(8,128)(2,1)S(1)}, u32[]{:S(2)}, u32[]{:S(2)}) collective-permute-start(bf16[16,512]{1,0:T(8,128)(2,1)S(1)} %convolution_convert_fusion.1), channel_id=1, source_target_pairs={{0,8},{4,12},{8,0},{12,4},{1,9},{5,13},{9,1},{13,5},{2,10},{6,14},... | collective-permute-start | bytes 49160 | tf_op jit(solution)/shard_map/ppermute | solution.py:157
  49.9 5.5 %collective-permute-start.5 = (bf16[16,512]{1,0:T(8,128)(2,1)S(1)}, bf16[16,512]{1,0:T(8,128)(2,1)S(1)}, u32[]{:S(2)}, u32[]{:S(2)}) collective-permute-start(bf16[16,512]{1,0:T(8,128)(2,1)S(1)} %convolution_convert_fusion.1), channel_id=1, source_target_pairs={{0,12},{4,8},{8,4},{12,0},{1,13},{5,9},{9,5},{13,1},{2,14},{6,10},... | collective-permute-start | bytes 49160 | tf_op jit(solution)/shard_map/ppermute | solution.py:157
  50.7 25.4 %copy-start.16 = (f32[8]{0:T(128)}, f32[8]{0:T(128)S(1)}, u32[]{:S(2)}) copy-start(f32[8]{0:T(128)S(1)} %select_reduce_fusion) | copy-start | bytes 100
  72.5 10.4 %all-to-all-start.1 = ((bf16[16,4,512]{2,1,0:T(4,128)(2,1)}), bf16[16,4,512]{2,1,0:T(4,128)(2,1)S(1)}, u32[]{:S(2)}, u32[]{:S(2)}) async-start(bf16[16,4,512]{2,1,0:T(4,128)(2,1)} %get-tuple-element.10), calls=%async_computation.1 | async-start | bytes 131072 | tf_op jit(solution)/shard_map/all_to_all | solution.py:294
  (9 other events, 42.7 us)

commit v3 on v2

--- a/solution.py
+++ b/solution.py
@@ -249,17 +249,17 @@
         state_index.reshape(1),
         *parts,
         step_gain[None],
-        in_vmem(step_proj),
+        step_proj,
         step_bias[None],
         decay_log,
-        in_vmem(ssm_state),
+        ssm_state,
         conv_out,
     )
     readout = jnp.sum(lax.all_gather(read_part, "state").astype(F32), axis=0)
     mixer_act = ((readout + skip_gain * conv_out) * jax.nn.silu(gate_branch)).astype(BF16)
 
     mixer_sum = exchange_sum(
-        jnp.dot(mixer_act, output_proj, preferred_element_type=F32), "head", BF16
+        jnp.dot(mixer_act, output_proj, preferred_element_type=F32), "head", F32
     )
     resid_cols = (tok_f32 + mixer_sum).astype(BF16)
     resid_all = lax.all_gather(resid_cols, "state", axis=1, tiled=True)

time: 85.1 us -> 85.3 us (level)
  no operation moved by 1% of the time
where the time goes in v3:
time: 85.3 us; the launch traced here: 84.9 us
  starting transfers between devices  18.7 us (22%)
  blocking collectives  18.6 us (22%)
  waiting for transfers between devices  17.2 us (20%)
  Pallas kernels  13.6 us (16%)
  local copies, waits for them, and re-layouts  6.49 us (8%)
  matrix products  4.62 us (5%)
  other arithmetic  2.91 us (3%)
  between operations  2.72 us (3%)
    pallas_call x1, Pallas kernels, per_device(): pl.pallas_call(experts_kernel, in_specs=[smem] + [vmem] * 6 + [pl.BlockSp...  11.7 us
    all_gather x1, blocking collectives, per_device(): branch_all = lax.all_gather(branch_sent, 'state').astype(F32)  7.48 us
    all_to_all x1, starting transfers between devices, gather_tokens(): lax.all_to_all(spread, axis, split_axis=0, concat_axis=0, tiled=True)  6.35 us
    unnamed x54, local copies, waits for them, and re-layouts  6.29 us
    all_gather x1, blocking collectives, per_device(): readout = jnp.sum(lax.all_gather(read_part, 'state').astype(F32), axis=0)  5.89 us
    all_to_all x1, waiting for transfers between devices, per_device(): lax.all_to_all(outgoing, ('head', 'state'), split_axis=0, concat_axis=0,...  5.57 us
    all_to_all x1, waiting for transfers between devices, gather_tokens(): lax.all_to_all(spread, axis, split_axis=0, concat_axis=0, tiled=True)  5.28 us
    all_gather x1, blocking collectives, per_device(): resid_all = lax.all_gather(resid_cols, 'state', axis=1, tiled=True)  5.24 us
  transfers between devices with their start and end apart: 8, of which 6 were waited for; matrix products, arithmetic and copies ran while one was open for 2% of the time, Pallas kernels for 0%

profile of v3, /device:TPU:0, one launch (start us, length us, event | category | flops | bytes accessed | tf_op | source)
XLA Modules:
  0.0 84.9 jit_solution(9577420137878450561)
XLA Ops:
  0.6 0.9 %copy.44.ids_ref = s32[4,2]{1,0:T(4,128)S(1)} copy(s32[4,2]{0,1:T(2,128)} %param.37) | data formatting | bytes 64 | tf_op args[16]
  1.6 0.8 copy.45.slot_ref
  2.3 0.7 copy-done.6
  3.0 0.7 pack.1
  3.7 6.3 %all-to-all-start = ((bf16[4,4,640]{2,1,0:T(4,128)(2,1)}), bf16[4,4,640]{2,1,0:T(4,128)(2,1)S(1)}, u32[]{:S(2)}, u32[]{:S(2)}) async-start(bf16[4,4,640]{2,1,0:T(4,128)(2,1)} %pack.1), calls=%async_computation | async-start | bytes 40960 | tf_op jit(solution)/shard_map/all_to_all | solution.py:54
  10.4 5.3 %all-to-all-done = bf16[4,4,640]{2,1,0:T(4,128)(2,1)S(1)} async-done(((bf16[4,4,640]{2,1,0:T(4,128)(2,1)}), bf16[4,4,640]{2,1,0:T(4,128)(2,1)S(1)}, u32[]{:S(2)}, u32[]{:S(2)}) %all-to-all-start) | async-done | bytes 20512 | tf_op jit(solution)/shard_map/all_to_all | solution.py:54
  15.9 2.8 %fusion = bf16[2,16,2048]{2,1,0:T(8,128)(2,1)S(1)} fusion(bf16[2,512,2048]{2,1,0:T(8,128)(2,1)} %param.23, f32[512]{0:T(512)S(1)} %copy-done.15, bf16[16,640]{1,0:T(8,128)(2,1)S(1)} %reshape.81), kind=kOutput, calls=%fused_computation.1 | convolution fusion | flops 67198976 | bytes 4343808 | tf_op jit(solution)/shard_map/td,kdc->ktc/dot_general | solution.py:218
  18.9 7.5 %all-gather = bf16[8,16,2176]{2,1,0:T(8,128)(2,1)S(1)} all-gather(bf16[2,16,2176]{2,1,0:T(8,128)(2,1)S(1)} %pad_maximum_fusion.1), channel_id=2, replica_groups=mesh['groups'=2,'head'=4,'state'=4] {'state'}, dimensions={0}, use_global_device_ids=true | all-gather | bytes 696320 | tf_op jit(solution)/shard_map/all_gather | solution.py:222
  27.6 0.7 collective-permute-start
  28.8 3.2 %collective-permute-start.2 = (f32[16,288]{1,0:T(8,128)S(1)}, f32[16,288]{1,0:T(8,128)S(1)}, u32[]{:S(2)}, u32[]{:S(2)}) collective-permute-start(f32[16,288]{1,0:T(8,128)S(1)} %fusion.8.proj_ref), channel_id=1, source_target_pairs={{0,12},{4,8},{8,4},{12,0},{1,13},{5,9},{9,5},{13,1},{2,14},{6,10},... | collective-permute-start | bytes 55304 | tf_op jit(solution)/shard_map/ppermute | solution.py:168
  32.0 0.8 fusion.3
  33.5 1.0 %collective-permute-done.2.refs_2_ = f32[16,288]{1,0:T(8,128)S(1)} collective-permute-done((f32[16,288]{1,0:T(8,128)S(1)}, f32[16,288]{1,0:T(8,128)S(1)}, u32[]{:S(2)}, u32[]{:S(2)}) %collective-permute-start.2) | collective-permute-done | bytes 18464 | tf_op jit(solution)/shard_map/ppermute | solution.py:168
  34.5 1.4 %copy-done.2 = bf16[256,2048]{1,0:T(8,128)(2,1)S(1)} copy-done((bf16[256,2048]{1,0:T(8,128)(2,1)S(1)}, bf16[256,2048]{1,0:T(8,128)(2,1)}, u32[]{:S(2)}) %copy-start.2) | copy-done | bytes 1048600
  35.9 1.7 %copy-done.3 = f32[4,16,2048]{2,1,0:T(8,128)S(1)} copy-done((f32[4,16,2048]{2,1,0:T(8,128)S(1)}, f32[4,16,2048]{2,1,0:T(8,128)}, u32[]{:S(2)}) %copy-start.3) | copy-done | bytes 524312
  37.6 1.3 %state_step.1 = (f32[4,16,2048]{2,1,0:T(8,128)}, bf16[16,2048]{1,0:T(8,128)(2,1)S(1)}) custom-call(s32[1]{0:T(128)} %bitcast.index_ref, f32[16,288]{1,0:T(8,128)S(1)} %fusion.8.proj_ref, f32[16,288]{1,0:T(8,128)S(1)} %collective-permute-done.refs_0_, f32[16,288]{1,0:T(8,128)S(1)} %collective-permute-done.1.refs_1_, ...), custom_call_target="tpu_custom_call" | custom-call | flops 20000000000 | bytes 100000000 | tf_op jit(solution)/shard_map/state_step/pallas_call | solution.py:236
  38.9 5.9 %all-gather.1 = bf16[64,2048]{1,0:T(8,128)(2,1)S(1)} all-gather(bf16[16,2048]{1,0:T(8,128)(2,1)S(1)} %get-tuple-element.9), channel_id=3, replica_groups=mesh['groups'=2,'head'=4,'state'=4] {'state'}, dimensions={0}, use_global_device_ids=true | all-gather | bytes 327680 | tf_op jit(solution)/shard_map/all_gather | solution.py:258
  44.8 1.3 %fusion.5 = f32[16,512]{1,0:T(8,128)S(1)} fusion(bf16[2048,512]{1,0:T(8,128)(2,1)S(1)} %copy-done, f32[2,16,2176]{2,1,0:T(8,128)} %copy-done.10, f32[16,2048]{1,0:T(8,128)S(1)} %convert_reduce_fusion.1, f32[16,2048]{1,0:T(8,128)S(1)} %divide_multiply_fusion.refs_8_, f32[16]{0:T(128)S(1)} %fusion.21, f32[2048]{0:T(1024)S(1)} %copy-done.13), kind=kOutput, calls=%fused_computation.17 | convolution fusion | flops 33849344 | bytes 2531392 | tf_op jit(solution)/shard_map/dot_general | solution.py:262
  46.3 3.7 %collective-permute-start.4 = (f32[16,512]{1,0:T(8,128)S(1)}, f32[16,512]{1,0:T(8,128)S(1)}, u32[]{:S(2)}, u32[]{:S(2)}) collective-permute-start(f32[16,512]{1,0:T(8,128)S(1)} %fusion.5), channel_id=1, source_target_pairs={{0,8},{4,12},{8,0},{12,4},{1,9},{5,13},{9,1},{13,5},{2,10},{6,14},... | collective-permute-start | bytes 98312 | tf_op jit(solution)/shard_map/ppermute | solution.py:157
  50.7 1.3 %collective-permute-done.4 = f32[16,512]{1,0:T(8,128)S(1)} collective-permute-done((f32[16,512]{1,0:T(8,128)S(1)}, f32[16,512]{1,0:T(8,128)S(1)}, u32[]{:S(2)}, u32[]{:S(2)}) %collective-permute-start.4) | collective-permute-done | bytes 32800 | tf_op jit(solution)/shard_map/ppermute | solution.py:157
  52.0 3.7 %collective-permute-done.5 = f32[16,512]{1,0:T(8,128)S(1)} collective-permute-done((f32[16,512]{1,0:T(8,128)S(1)}, f32[16,512]{1,0:T(8,128)S(1)}, u32[]{:S(2)}, u32[]{:S(2)}) %collective-permute-start.5) | collective-permute-done | bytes 32800 | tf_op jit(solution)/shard_map/ppermute | solution.py:157
  55.7 5.2 %all_gather.19.resid_ref = bf16[16,2048]{1,0:T(8,128)(2,1)S(1)} all-gather(bf16[16,512]{1,0:T(8,128)(2,1)S(1)} %fusion.13), channel_id=1, replica_groups=mesh['groups'=2,'head'=4,'state'=4] {'state'}, dimensions={1}, use_global_device_ids=true | all-gather | bytes 81920 | tf_op jit(solution)/shard_map/all_gather | solution.py:265
  61.0 11.7 %experts.1 = (bf16[16,4,512]{2,1,0:T(4,128)(2,1)}, f32[16,8]{1,0:T(8,128)S(1)}) custom-call(s32[2]{0:T(128)S(1)} %iota_add_fusion.own_ref, bf16[16,2048]{1,0:T(8,128)(2,1)S(1)} %all_gather.19.resid_ref, bf16[16,128]{1,0:T(8,128)(2,1)S(1)} %slice.41.route_ref, f32[1,2048]{1,0:T(1,128)S(1)} %bitcast.35, f32[2048,8]{1,0:T(8,128)S(1)} %copy.47.router_ref, ...), custom_call_target="tpu_custom_call" | custom-call | tf_op jit(solution)/shard_map/experts/pallas_call | solution.py:269
  72.7 3.5 %all-to-all-start.1 = ((bf16[16,4,512]{2,1,0:T(4,128)(2,1)}), bf16[16,4,512]{2,1,0:T(4,128)(2,1)S(1)}, u32[]{:S(2)}, u32[]{:S(2)}) async-start(bf16[16,4,512]{2,1,0:T(4,128)(2,1)} %get-tuple-element.10), calls=%async_computation.1 | async-start | bytes 131072 | tf_op jit(solution)/shard_map/all_to_all | solution.py:294
  77.5 5.6 %all-to-all-done.1 = bf16[16,4,512]{2,1,0:T(4,128)(2,1)S(1)} async-done(((bf16[16,4,512]{2,1,0:T(4,128)(2,1)}), bf16[16,4,512]{2,1,0:T(4,128)(2,1)S(1)}, u32[]{:S(2)}, u32[]{:S(2)}) %all-to-all-start.1) | async-done | bytes 65568 | tf_op jit(solution)/shard_map/all_to_all | solution.py:294
  (84 shorter events, 5.3 us)
Async XLA Ops:
  0.6 44.2 %copy-start = (bf16[2048,512]{1,0:T(8,128)(2,1)S(1)}, bf16[2048,512]{1,0:T(8,128)(2,1)}, u32[]{:S(2)}) copy-start(bf16[2048,512]{1,0:T(8,128)(2,1)} %param.34) | copy-start | bytes 6291460
  3.0 12.9 %copy-start.15 = (f32[512]{0:T(512)S(1)}, f32[512]{0:T(512)}, u32[]{:S(2)}) copy-start(f32[512]{0:T(512)} %param.22) | copy-start | bytes 6148
  3.7 12.0 %all-to-all-start = ((bf16[4,4,640]{2,1,0:T(4,128)(2,1)}), bf16[4,4,640]{2,1,0:T(4,128)(2,1)S(1)}, u32[]{:S(2)}, u32[]{:S(2)}) async-start(bf16[4,4,640]{2,1,0:T(4,128)(2,1)} %pack.1), calls=%async_computation | async-start | bytes 40960 | tf_op jit(solution)/shard_map/all_to_all | solution.py:54
  18.8 8.3 %copy-start.14 = (f32[2048]{0:T(1024)S(1)}, f32[2048]{0:T(1024)}, u32[]{:S(2)}) copy-start(f32[2048]{0:T(1024)} %param.25) | copy-start | bytes 24580
  18.8 8.4 %copy-start.9 = (bf16[2048,288]{0,1:T(8,128)(2,1)S(1)}, bf16[2048,288]{0,1:T(8,128)(2,1)}, u32[]{:S(2)}) copy-start(bf16[2048,288]{0,1:T(8,128)(2,1)} %param.27) | copy-start | bytes 3538948
  26.3 8.1 %copy-start.5 = (f32[2048]{0:T(1024)S(1)}, f32[2048]{0:T(1024)}, u32[]{:S(2)}) copy-start(f32[2048]{0:T(1024)} %param.30) | copy-start | bytes 24580
  26.3 8.1 %copy-start.7 = (f32[256]{0:T(256)S(1)}, f32[256]{0:T(256)}, u32[]{:S(2)}) copy-start(f32[256]{0:T(256)} %param.28) | copy-start | bytes 3076
  27.6 5.4 %collective-permute-start = (f32[16,288]{1,0:T(8,128)S(1)}, f32[16,288]{1,0:T(8,128)S(1)}, u32[]{:S(2)}, u32[]{:S(2)}) collective-permute-start(f32[16,288]{1,0:T(8,128)S(1)} %fusion.8.proj_ref), channel_id=1, source_target_pairs={{0,4},{4,0},{8,12},{12,8},{1,5},{5,1},{9,13},{13,9},{2,6},{6,2},{1... | collective-permute-start | bytes 55304 | tf_op jit(solution)/shard_map/ppermute | solution.py:168
  28.3 5.1 %collective-permute-start.1 = (f32[16,288]{1,0:T(8,128)S(1)}, f32[16,288]{1,0:T(8,128)S(1)}, u32[]{:S(2)}, u32[]{:S(2)}) collective-permute-start(f32[16,288]{1,0:T(8,128)S(1)} %fusion.8.proj_ref), channel_id=1, source_target_pairs={{0,8},{4,12},{8,0},{12,4},{1,9},{5,13},{9,1},{13,5},{2,10},{6,14},... | collective-permute-start | bytes 55304 | tf_op jit(solution)/shard_map/ppermute | solution.py:168
  28.8 5.6 %collective-permute-start.2 = (f32[16,288]{1,0:T(8,128)S(1)}, f32[16,288]{1,0:T(8,128)S(1)}, u32[]{:S(2)}, u32[]{:S(2)}) collective-permute-start(f32[16,288]{1,0:T(8,128)S(1)} %fusion.8.proj_ref), channel_id=1, source_target_pairs={{0,12},{4,8},{8,4},{12,0},{1,13},{5,9},{9,5},{13,1},{2,14},{6,10},... | collective-permute-start | bytes 55304 | tf_op jit(solution)/shard_map/ppermute | solution.py:168
  34.5 26.4 %slice-start = ((s8[14680064]{0:T(1024)(128)(4,1)}), s8[4194304]{0:T(1024)(128)(4,1)S(1)}, s32[]{:S(2)}) async-start(s8[14680064]{0:T(1024)(128)(4,1)} %bitcast.31), calls=%async_computation.2 | async-start | bytes 8388608
  34.5 26.4 %slice-start.4 = ((s8[14680064]{0:T(1024)(128)(4,1)}), s8[4194304]{0:T(1024)(128)(4,1)S(1)}, s32[]{:S(2)}) async-start(s8[14680064]{0:T(1024)(128)(4,1)} %bitcast.33), calls=%async_computation.6 | async-start | bytes 8388608
  37.6 23.3 %slice-start.1 = ((s8[14680064]{0:T(1024)(128)(4,1)}), s8[4194304]{0:T(1024)(128)(4,1)S(1)}, s32[]{:S(2)}) async-start(s8[14680064]{0:T(1024)(128)(4,1)} %bitcast.31), calls=%async_computation.3 | async-start | bytes 8388608
  37.6 23.3 %slice-start.2 = ((s8[14680064]{0:T(1024)(128)(4,1)}), s8[4194304]{0:T(1024)(128)(4,1)S(1)}, s32[]{:S(2)}) async-start(s8[14680064]{0:T(1024)(128)(4,1)} %bitcast.31), calls=%async_computation.4 | async-start | bytes 8388608
  37.6 23.4 %slice-start.3 = ((s8[14680064]{0:T(1024)(128)(4,1)}), s8[2097152]{0:T(1024)(128)(4,1)S(1)}, s32[]{:S(2)}) async-start(s8[14680064]{0:T(1024)(128)(4,1)} %bitcast.31), calls=%async_computation.5 | async-start | bytes 4194304
  37.6 23.4 %slice-start.5 = ((s8[14680064]{0:T(1024)(128)(4,1)}), s8[4194304]{0:T(1024)(128)(4,1)S(1)}, s32[]{:S(2)}) async-start(s8[14680064]{0:T(1024)(128)(4,1)} %bitcast.33), calls=%async_computation.7 | async-start | bytes 8388608
  37.6 23.4 %slice-start.6 = ((s8[14680064]{0:T(1024)(128)(4,1)}), s8[4194304]{0:T(1024)(128)(4,1)S(1)}, s32[]{:S(2)}) async-start(s8[14680064]{0:T(1024)(128)(4,1)} %bitcast.33), calls=%async_computation.8 | async-start | bytes 8388608
  37.6 23.4 %slice-start.7 = ((s8[14680064]{0:T(1024)(128)(4,1)}), s8[2097152]{0:T(1024)(128)(4,1)S(1)}, s32[]{:S(2)}) async-start(s8[14680064]{0:T(1024)(128)(4,1)} %bitcast.33), calls=%async_computation.9 | async-start | bytes 4194304
  38.9 22.1 %copy-start.1 = (f32[2048]{0:T(1024)S(1)}, f32[2048]{0:T(1024)}, u32[]{:S(2)}) copy-start(f32[2048]{0:T(1024)} %param.35) | copy-start | bytes 24580
  46.2 4.5 %collective-permute-start.3 = (f32[16,512]{1,0:T(8,128)S(1)}, f32[16,512]{1,0:T(8,128)S(1)}, u32[]{:S(2)}, u32[]{:S(2)}) collective-permute-start(f32[16,512]{1,0:T(8,128)S(1)} %fusion.5), channel_id=1, source_target_pairs={{0,4},{4,0},{8,12},{12,8},{1,5},{5,1},{9,13},{13,9},{2,6},{6,2},{1... | collective-permute-start | bytes 98312 | tf_op jit(solution)/shard_map/ppermute | solution.py:157
  46.3 5.7 %collective-permute-start.4 = (f32[16,512]{1,0:T(8,128)S(1)}, f32[16,512]{1,0:T(8,128)S(1)}, u32[]{:S(2)}, u32[]{:S(2)}) collective-permute-start(f32[16,512]{1,0:T(8,128)S(1)} %fusion.5), channel_id=1, source_target_pairs={{0,8},{4,12},{8,0},{12,4},{1,9},{5,13},{9,1},{13,5},{2,10},{6,14},... | collective-permute-start | bytes 98312 | tf_op jit(solution)/shard_map/ppermute | solution.py:157
  49.9 5.7 %collective-permute-start.5 = (f32[16,512]{1,0:T(8,128)S(1)}, f32[16,512]{1,0:T(8,128)S(1)}, u32[]{:S(2)}, u32[]{:S(2)}) collective-permute-start(f32[16,512]{1,0:T(8,128)S(1)} %fusion.5), channel_id=1, source_target_pairs={{0,12},{4,8},{8,4},{12,0},{1,13},{5,9},{9,5},{13,1},{2,14},{6,10},... | collective-permute-start | bytes 98312 | tf_op jit(solution)/shard_map/ppermute | solution.py:157
  50.7 25.6 %copy-start.16 = (f32[8]{0:T(128)}, f32[8]{0:T(128)S(1)}, u32[]{:S(2)}) copy-start(f32[8]{0:T(128)S(1)} %select_reduce_fusion) | copy-start | bytes 100
  72.7 10.4 %all-to-all-start.1 = ((bf16[16,4,512]{2,1,0:T(4,128)(2,1)}), bf16[16,4,512]{2,1,0:T(4,128)(2,1)S(1)}, u32[]{:S(2)}, u32[]{:S(2)}) async-start(bf16[16,4,512]{2,1,0:T(4,128)(2,1)} %get-tuple-element.10), calls=%async_computation.1 | async-start | bytes 131072 | tf_op jit(solution)/shard_map/all_to_all | solution.py:294
  (9 other events, 42.7 us)
